TPU v7x, 128 devices: a whole 4x4x4 slice. The times are simulated.
128 devices in a mesh: wide: 16 (over x, y), narrow: 8 (over z, core).
Axes of the slice: x: 4, y: 4, z: 4, core: 2. Of those that a mesh axis runs over, the one named last changes fastest.
Arguments:
- old_field: float32 [4096, 128, 128], P(('wide', 'narrow')), may hold values from -6 to 6
- old_level: int32 [4096], P(('wide', 'narrow')), may hold values from 0 to 1
- new_source: int32 [32, 32], P('wide', 'narrow'), may hold values from 0 to 4095, as said below
- stretch_coef: float32 [8192, 8192], P('wide', 'narrow'), may hold values from 0.2 to 2
- bend_coef: float32 [8192, 8192], P('wide', 'narrow'), may hold values from 0.05 to 0.5
- load_field: float32 [8192, 8192], P('wide', 'narrow'), may hold values from -6 to 6
Outputs:
- relaxed: float32 [8192, 8192], P('wide', 'narrow')
Inputs may be any that keep to these rules, and one draw needn't show every extreme that they name: new_source names an old block held by a device with the same narrow index; one old device gives at most 2 sibling groups to one new device, and exactly 2 wherever it gives any.
All inputs are finite; a program needn't handle non-finite values.
Results may differ from a plain program's by a relative error of at most 0.0001.
Values sent between devices are 32-bit elements; how exact they have to be, the bound alone decides.
No kernel may reach another device: no remote copies, remote signals or barrier semaphores. Data moves between devices by JAX's collectives and lax.ppermute only.
A program may use at most 128 MiB of HBM per device.

v0:
```python
import jax
import jax.numpy as jnp
from jax import lax
from jax.sharding import PartitionSpec as P

SWEEPS = 2


OMEGA = 0.5


def in_order(tiles, dim):
    tiles = jnp.moveaxis(tiles, 0, dim)
    shape = tiles.shape
    return tiles.reshape(*shape[:dim], shape[dim] * shape[dim + 1], *shape[dim + 2 :])


def sent_to_all(shard, axis):
    count = lax.axis_size(axis)
    return lax.all_to_all(
        jnp.broadcast_to(shard[None], (count, *shard.shape)), axis, 0, 0, tiled=True
    )


def collect(shard, axis, dim):
    return in_order(sent_to_all(shard, axis), dim)


def padded_2(cells, sides, width):
    for axis, dim in sides:
        count = lax.axis_size(axis)
        ends = count - 1
        head = lax.slice_in_dim(cells, 0, width, axis=dim)
        tail = lax.slice_in_dim(cells, cells.shape[dim] - width, cells.shape[dim], axis=dim)
        cells = jnp.concatenate(
            [
                lax.ppermute(tail, axis, [(i, (i + 1) % count) for i in range(ends)]),
                cells,
                lax.ppermute(head, axis, [((i + 1) % count, i) for i in range(ends)]),
            ],
            axis=dim,
        )
    return cells


def quadrant_table(side_cells, half_index):
    half_size = side_cells // 2
    row_ids = jnp.arange(side_cells, dtype=jnp.int32)[:, None]
    col_ids = jnp.arange(side_cells, dtype=jnp.int32)[None, :]
    base_cell = half_index * half_size
    near_cell = base_cell + row_ids // 2
    other_cell = near_cell + jnp.where(row_ids % 2 == 1, 1, -1)
    other_cell = jnp.clip(other_cell, base_cell, base_cell + half_size - 1)
    return 0.75 * (col_ids == near_cell).astype(jnp.float32) + 0.25 * (
        col_ids == other_cell
    ).astype(jnp.float32)


def refine_group(parents):
    side_cells = parents.shape[-1]
    tables = [quadrant_table(side_cells, 0), quadrant_table(side_cells, 1)]
    upper = [
        jnp.einsum("ij,njk->nik", table, parents, precision=lax.Precision.HIGHEST)
        for table in tables
    ]
    rows_out = []
    for half_x in range(2):
        pair = [
            jnp.einsum(
                "nik,lk->nil", upper[half_x], tables[half_y], precision=lax.Precision.HIGHEST
            )
            for half_y in range(2)
        ]
        rows_out.append(jnp.stack(pair, axis=1))
    return jnp.stack(rows_out, axis=1)


def spacing_factor(levels):
    return 1.0 + 3.0 * (levels >= 1).astype(jnp.float32)


def relax(field_pad, stretch_pad, bend_pad, load_core, inside):
    center = field_pad[2:-2, 2:-2]
    laplace = (
        field_pad[:-2, 1:-1]
        + field_pad[2:, 1:-1]
        + field_pad[1:-1, :-2]
        + field_pad[1:-1, 2:]
        - 4.0 * field_pad[1:-1, 1:-1]
    )
    moment = bend_pad * laplace
    bending = (
        moment[:-2, 1:-1]
        + moment[2:, 1:-1]
        + moment[1:-1, :-2]
        + moment[1:-1, 2:]
        - 4.0 * moment[1:-1, 1:-1]
    )
    stretch_mid = stretch_pad[1:-1, 1:-1]
    diagonal = 16.0 * bend_pad[1:-1, 1:-1]
    stretching = jnp.zeros_like(center)
    neighbours = (
        (stretch_pad[:-2, 1:-1], bend_pad[:-2, 1:-1], field_pad[1:-3, 2:-2]),
        (stretch_pad[2:, 1:-1], bend_pad[2:, 1:-1], field_pad[3:-1, 2:-2]),
        (stretch_pad[1:-1, :-2], bend_pad[1:-1, :-2], field_pad[2:-2, 1:-3]),
        (stretch_pad[1:-1, 2:], bend_pad[1:-1, 2:], field_pad[2:-2, 3:-1]),
    )
    for near_stretch, near_bend, near_field in neighbours:
        face_coef = 0.5 * (stretch_mid + near_stretch)
        stretching = stretching + face_coef * (center - near_field)
        diagonal = diagonal + face_coef + near_bend
    remainder = load_core - (stretching + bending)
    if inside is None:
        return center + OMEGA * remainder / diagonal
    safe_diag = jnp.where(inside, diagonal, 1.0)
    return jnp.where(inside, center + OMEGA * remainder / safe_diag, 0.0)


def local(old_field, old_level, new_source, stretch_coef, bend_coef, load_field):
    per_device = old_field.shape[0]
    side_cells = old_field.shape[1]
    groups_x, groups_y = new_source.shape
    per_groups = groups_x * groups_y
    wide_count = lax.axis_size("wide")
    segments = lax.axis_size("narrow")
    my_rank = lax.axis_index("wide")
    capacity = max(2, per_groups // wide_count)
    route_table = collect(new_source, "wide", 0)
    all_source = route_table.reshape(wide_count, per_groups)
    from_rank = all_source // per_device // segments
    from_local = all_source % per_device
    positions = jnp.arange(per_groups, dtype=jnp.int32)
    earlier = (positions[None, :] < positions[:, None]).astype(jnp.int32)
    same_rank = (from_rank[:, :, None] == from_rank[:, None, :]).astype(jnp.int32)
    slot_ids = jnp.sum(same_rank * earlier[None, :, :], axis=2)
    slot_range = jnp.arange(capacity, dtype=jnp.int32)
    chosen = (
        (from_rank[:, None, :] == my_rank) & (slot_ids[:, None, :] == slot_range[None, :, None])
    ).astype(jnp.int32)
    pick_local = jnp.sum(chosen * from_local[:, None, :], axis=2).reshape(-1)
    parents = old_field[pick_local]
    parent_spacing = spacing_factor(old_level[pick_local])
    own_index = from_rank[my_rank] * capacity + slot_ids[my_rank]
    arrived, arrived_spacing = (
        lax.all_to_all(
            parents.reshape(wide_count, capacity, side_cells, side_cells),
            "wide",
            split_axis=0,
            concat_axis=0,
            tiled=True,
        ),
        lax.all_to_all(
            parent_spacing.reshape(wide_count, capacity),
            "wide",
            split_axis=0,
            concat_axis=0,
            tiled=True,
        ),
    )
    blocks = refine_group(arrived.reshape(-1, side_cells, side_cells)[own_index])
    spacing = arrived_spacing.reshape(-1)[own_index]
    rows_here = groups_x * 2 * side_cells
    cols_here = groups_y * 2 * side_cells
    grid_field = (
        blocks.reshape(groups_x, groups_y, 2, 2, side_cells, side_cells)
        .transpose(0, 2, 4, 1, 3, 5)
        .reshape(rows_here, cols_here)
    )
    scale_grid = jnp.repeat(
        jnp.repeat(spacing.reshape(groups_x, groups_y), 2 * side_cells, axis=0),
        2 * side_cells,
        axis=1,
    )
    stretch_eff = stretch_coef * scale_grid
    bend_eff = bend_coef * scale_grid * scale_grid
    coef_depth = 2 * SWEEPS - 1
    coeffs = padded_2(
        jnp.stack([stretch_eff, bend_eff, load_field]), (("wide", 1), ("narrow", 2)), coef_depth
    )
    padded = padded_2(grid_field, (("wide", 0), ("narrow", 1)), 2 * SWEEPS)
    row_start = my_rank * rows_here
    col_start = lax.axis_index("narrow") * cols_here
    total_rows = rows_here * wide_count
    total_cols = cols_here * segments
    full_rows = coeffs.shape[1]
    full_cols = coeffs.shape[2]
    for sweep_index in range(SWEEPS):
        rim_cells = 2 * (SWEEPS - 1 - sweep_index)
        coef_cut = coef_depth - rim_cells - 1
        load_cut = coef_depth - rim_cells
        stretch_pad = coeffs[0, coef_cut : full_rows - coef_cut, coef_cut : full_cols - coef_cut]
        bend_pad = coeffs[1, coef_cut : full_rows - coef_cut, coef_cut : full_cols - coef_cut]
        load_core = coeffs[2, load_cut : full_rows - load_cut, load_cut : full_cols - load_cut]
        if rim_cells > 0:
            row_global = (
                row_start - rim_cells + jnp.arange(rows_here + 2 * rim_cells, dtype=jnp.int32)
            )
            col_global = (
                col_start - rim_cells + jnp.arange(cols_here + 2 * rim_cells, dtype=jnp.int32)
            )
            inside = ((row_global >= 0) & (row_global < total_rows))[:, None] & (
                (col_global >= 0) & (col_global < total_cols)
            )[None, :]
            padded = relax(padded, stretch_pad, bend_pad, load_core, inside)
        else:
            padded = relax(padded, stretch_pad, bend_pad, load_core, None)
    grid_field = padded
    return grid_field


def solution(mesh):
    return jax.shard_map(
        local,
        mesh=mesh,
        in_specs=(
            P(("wide", "narrow"), None, None),
            P(("wide", "narrow")),
            P("wide", "narrow"),
            P("wide", "narrow"),
            P("wide", "narrow"),
            P("wide", "narrow"),
        ),
        out_specs=P("wide", "narrow"),
        check_vma=False,
    )
```

profile of v0, /device:TPU:7, one launch (start us, length us, event | category | flops | bytes accessed | tf_op | source)
XLA Modules:
  0.0 180.7 jit_solution(14362249715421543916)
XLA Ops:
  0.0 1.4 broadcast_in_dim.16
  1.4 6.9 %all-to-all-start = ((s32[16,2,4]{2,1,0:T(2,128)}), s32[16,2,4]{2,1,0:T(2,128)S(1)}, u32[]{:S(2)}, u32[]{:S(2)}) async-start(s32[16,2,4]{2,1,0:T(2,128)} %broadcast_in_dim.16), calls=%async_computation | async-start | bytes 32768 | tf_op jit(solution)/shard_map/all_to_all | solution.py:20
  8.3 4.7 %all-to-all-done = s32[16,2,4]{2,1,0:T(2,128)S(1)} async-done(((s32[16,2,4]{2,1,0:T(2,128)}), s32[16,2,4]{2,1,0:T(2,128)S(1)}, u32[]{:S(2)}, u32[]{:S(2)}) %all-to-all-start) | async-done | bytes 544 | tf_op jit(solution)/shard_map/all_to_all | solution.py:20
  13.5 1.4 gather_fusion.2
  15.6 5.1 %all-to-all-start.2 = ((f32[16,1,2]{2,1,0:T(1,128)}), f32[16,1,2]{2,1,0:T(1,128)S(1)}, u32[]{:S(2)}, u32[]{:S(2)}) async-start(f32[16,1,2]{2,1,0:T(1,128)} %bitcast.14), calls=%async_computation.2 | async-start | bytes 16384 | tf_op jit(solution)/shard_map/all_to_all | solution.py:152
  20.7 2.0 %gather_fusion = f32[32,128,128]{2,1,0:T(8,128)} fusion(f32[32,128,128]{2,1,0:T(8,128)S(1)} %copy-done, s32[1024]{0:T(1024)S(1)} %pad_clamp_fusion.1), kind=kCustom, calls=%fused_computation | custom fusion | bytes 4194432 | tf_op jit(solution)/shard_map/gather | solution.py:141
  22.7 2.6 %all-to-all-done.2 = f32[16,1,2]{2,1,0:T(1,128)S(1)} async-done(((f32[16,1,2]{2,1,0:T(1,128)}), f32[16,1,2]{2,1,0:T(1,128)S(1)}, u32[]{:S(2)}, u32[]{:S(2)}) %all-to-all-start.2) | async-done | bytes 160 | tf_op jit(solution)/shard_map/all_to_all | solution.py:152
  25.3 6.0 %all-to-all-start.1 = ((f32[16,2,128,128]{3,2,1,0:T(8,128)}), f32[16,2,128,128]{3,2,1,0:T(8,128)}, u32[]{:S(2)}, u32[]{:S(2)}) async-start(f32[16,2,128,128]{3,2,1,0:T(8,128)} %bitcast.69), calls=%async_computation.1 | async-start | bytes 4194304 | tf_op jit(solution)/shard_map/all_to_all | solution.py:145
  39.6 3.1 %collective-permute-start.4 = (f32[3,3,1024]{2,1,0:T(4,128)S(1)}, f32[3,3,1024]{2,1,0:T(4,128)S(1)}, u32[]{:S(2)}, u32[]{:S(2)}) collective-permute-start(f32[3,3,1024]{2,1,0:T(4,128)S(1)} %get-tuple-element.13), channel_id=1, source_target_pairs={{0,8},{8,16},{16,24},{24,32},{32,40},{40,48},{48,56},{56,64},{64,7... | collective-permute-start | bytes 110600 | tf_op jit(solution)/shard_map/ppermute | solution.py:37
  42.7 4.3 %collective-permute-start.5 = (f32[3,3,1024]{2,1,0:T(4,128)S(1)}, f32[3,3,1024]{2,1,0:T(4,128)S(1)}, u32[]{:S(2)}, u32[]{:S(2)}) collective-permute-start(f32[3,3,1024]{2,1,0:T(4,128)S(1)} %get-tuple-element.14), channel_id=1, source_target_pairs={{8,0},{16,8},{24,16},{32,24},{40,32},{48,40},{56,48},{64,56},{72,6... | collective-permute-start | bytes 110600 | tf_op jit(solution)/shard_map/ppermute | solution.py:39
  47.0 8.4 %collective-permute-done.4 = f32[3,3,1024]{2,1,0:T(4,128)S(1)} collective-permute-done((f32[3,3,1024]{2,1,0:T(4,128)S(1)}, f32[3,3,1024]{2,1,0:T(4,128)S(1)}, u32[]{:S(2)}, u32[]{:S(2)}) %collective-permute-start.4) | collective-permute-done | bytes 36896 | tf_op jit(solution)/shard_map/ppermute | solution.py:37
  55.9 2.7 %pad_maximum_fusion = f32[3,518,1024]{2,1,0:T(8,128)S(1)} fusion(f32[3,3,1024]{2,1,0:T(4,128)S(1)} %collective-permute-done.5, f32[1,512,1024]{2,1,0:T(8,128)S(1)} %bitcast.67, f32[1,512,1024]{2,1,0:T(8,128)} %copy-done.8, f32[1,512,1024]{2,1,0:T(8,128)} %copy-done.7, f32[3,3,1024]{2,1,0:T(4,128)S(1)} %collective-permute-done.4), kind=kLoop, calls=%fused_computation.4 | loop fusion | flops 6365184 | bytes 12730368 | tf_op jit(solution)/shard_map/concatenate | solution.py:35
  58.6 2.8 %copy-done.5 = f32[3,518,1024]{2,1,0:T(8,128)} copy-done((f32[3,518,1024]{2,1,0:T(8,128)}, f32[3,518,1024]{2,1,0:T(8,128)S(1)}, u32[]{:S(2)}) %copy-start.5) | copy-done | bytes 6365208
  62.0 8.1 %collective-permute-start.6 = (f32[3,518,3]{1,2,0:T(4,128)S(1)}, f32[3,518,3]{1,2,0:T(4,128)S(1)}, u32[]{:S(2)}, u32[]{:S(2)}) collective-permute-start(f32[3,518,3]{1,2,0:T(4,128)S(1)} %copy.77), channel_id=1, source_target_pairs={{0,1},{1,2},{2,3},{3,4},{4,5},{5,6},{6,7},{8,9},{9,10},{10,11},{11... | collective-permute-start | bytes 55952 | tf_op jit(solution)/shard_map/ppermute | solution.py:37
  70.4 2.1 %collective-permute-start.7 = (f32[3,518,3]{1,2,0:T(4,128)S(1)}, f32[3,518,3]{1,2,0:T(4,128)S(1)}, u32[]{:S(2)}, u32[]{:S(2)}) collective-permute-start(f32[3,518,3]{1,2,0:T(4,128)S(1)} %copy.78), channel_id=1, source_target_pairs={{1,0},{2,1},{3,2},{4,3},{5,4},{6,5},{7,6},{9,8},{10,9},{11,10},{12... | collective-permute-start | bytes 55952 | tf_op jit(solution)/shard_map/ppermute | solution.py:39
  72.8 2.8 %collective-permute-done.7 = f32[3,518,3]{1,2,0:T(4,128)S(1)} collective-permute-done((f32[3,518,3]{1,2,0:T(4,128)S(1)}, f32[3,518,3]{1,2,0:T(4,128)S(1)}, u32[]{:S(2)}, u32[]{:S(2)}) %collective-permute-start.7) | collective-permute-done | bytes 18680 | tf_op jit(solution)/shard_map/ppermute | solution.py:39
  75.9 9.1 %concatenate.18 = f32[3,518,1030]{2,1,0:T(8,128)} concatenate(f32[3,518,3]{2,1,0:T(8,128)S(1)} %copy.79, f32[3,518,1024]{2,1,0:T(8,128)} %copy-done.5, f32[3,518,3]{2,1,0:T(8,128)S(1)} %copy.80), dimensions={2} | concatenate | bytes 12804960 | tf_op jit(solution)/shard_map/concatenate | solution.py:35
  85.0 2.2 %gather_fusion.1 = f32[8,128,128]{2,1,0:T(8,128)S(1)} fusion(f32[32,128,128]{2,1,0:T(8,128)} %bitcast.3, s32[1024]{0:T(1024)S(1)} %pad_clamp_fusion), kind=kCustom, calls=%fused_computation.1 | custom fusion | bytes 1048608 | tf_op jit(solution)/shard_map/gather | solution.py:160
  93.7 2.9 %copy.75 = f32[2,2,128,4,2,128]{5,4,3,2,1,0:T(2,128)} copy(f32[2,2,128,4,2,128]{5,2,3,0,4,1:T(8,128)S(1)} %maximum_bitcast_fusion) | data formatting | bytes 4194304 | tf_op jit(solution)/shard_map/transpose | solution.py:166
  96.6 2.9 %reshape.343 = f32[512,1024]{1,0:T(8,128)S(1)} reshape(f32[2,2,128,4,2,128]{5,4,3,2,1,0:T(2,128)} %copy.75) | data formatting | bytes 4194304 | tf_op jit(solution)/shard_map/reshape | solution.py:167
  99.6 1.9 %collective-permute-start = (f32[4,1024]{1,0:T(4,128)S(1)}, f32[4,1024]{1,0:T(4,128)S(1)}, u32[]{:S(2)}, u32[]{:S(2)}) collective-permute-start(f32[4,1024]{1,0:T(4,128)S(1)} %get-tuple-element.17), channel_id=1, source_target_pairs={{0,8},{8,16},{16,24},{24,32},{32,40},{40,48},{48,56},{56,64},{64,7... | collective-permute-start | bytes 49160 | tf_op jit(solution)/shard_map/ppermute | solution.py:37
  101.5 5.7 %collective-permute-start.1 = (f32[4,1024]{1,0:T(4,128)S(1)}, f32[4,1024]{1,0:T(4,128)S(1)}, u32[]{:S(2)}, u32[]{:S(2)}) collective-permute-start(f32[4,1024]{1,0:T(4,128)S(1)} %get-tuple-element.18), channel_id=1, source_target_pairs={{8,0},{16,8},{24,16},{32,24},{40,32},{48,40},{56,48},{64,56},{72,6... | collective-permute-start | bytes 49160 | tf_op jit(solution)/shard_map/ppermute | solution.py:39
  107.3 4.8 %slice_bitcast_fusion.3 = (f32[518,1030]{1,0:T(8,128)}, f32[518,1030]{1,0:T(8,128)}) fusion(f32[3,518,1030]{2,1,0:T(8,128)} %concatenate.18), kind=kLoop, calls=%fused_computation.61 | loop fusion | bytes 8536640 | tf_op jit(solution)/shard_map/squeeze | solution.py:191
  113.9 2.5 %collective-permute-start.2 = (f32[520,4]{1,0:T(8,128)S(1)}, f32[520,4]{1,0:T(8,128)S(1)}, u32[]{:S(2)}, u32[]{:S(2)}) collective-permute-start(f32[520,4]{1,0:T(8,128)S(1)} %get-tuple-element.16), channel_id=1, source_target_pairs={{0,1},{1,2},{2,3},{3,4},{4,5},{5,6},{6,7},{8,9},{9,10},{10,11},{11... | collective-permute-start | bytes 24968 | tf_op jit(solution)/shard_map/ppermute | solution.py:37
  116.3 2.1 %collective-permute-start.3 = (f32[520,4]{1,0:T(8,128)S(1)}, f32[520,4]{1,0:T(8,128)S(1)}, u32[]{:S(2)}, u32[]{:S(2)}) collective-permute-start(f32[520,4]{1,0:T(8,128)S(1)} %get-tuple-element.15), channel_id=1, source_target_pairs={{1,0},{2,1},{3,2},{4,3},{5,4},{6,5},{7,6},{9,8},{10,9},{11,10},{12... | collective-permute-start | bytes 24968 | tf_op jit(solution)/shard_map/ppermute | solution.py:39
  118.5 4.0 %slice_bitcast_fusion.1 = (f32[514,1026]{1,0:T(8,128)}, f32[514,1026]{1,0:T(8,128)}) fusion(f32[3,518,1030]{2,1,0:T(8,128)S(1)} %bitcast.65), kind=kLoop, calls=%fused_computation.17 | loop fusion | bytes 8437824 | tf_op jit(solution)/shard_map/squeeze | solution.py:191
  122.6 1.5 collective-permute-done.3
  124.1 3.1 %concatenate.16 = f32[520,1032]{1,0:T(8,128)S(1)} concatenate(f32[520,4]{1,0:T(8,128)S(1)} %collective-permute-done.2, f32[520,1024]{1,0:T(8,128)} %copy-done.9, f32[520,4]{1,0:T(8,128)S(1)} %collective-permute-done.3), dimensions={1} | concatenate | bytes 4293120 | tf_op jit(solution)/shard_map/concatenate | solution.py:35
  127.2 4.4 %fusion.13 = f32[518,1030]{1,0:T(8,128)S(1)} fusion(f32[520,1032]{1,0:T(8,128)S(1)} %concatenate.16, f32[3,518,1030]{2,1,0:T(8,128)} %concatenate.18), kind=kLoop, calls=%fused_computation.37 | loop fusion | flops 3201240 | bytes 14939120 | tf_op jit(solution)/shard_map/mul | solution.py:91
  131.6 13.3 %and_select_fusion = f32[516,1028]{1,0:T(8,128)S(1)} fusion(f32[518,1030]{1,0:T(8,128)S(1)} %copy-done.4, f32[518,1030]{1,0:T(8,128)S(1)} %fusion.13, f32[520,1032]{1,0:T(8,128)S(1)} %concatenate.16, f32[518,1030]{1,0:T(8,128)S(1)} %copy-done.3, f32[3,518,1030]{2,1,0:T(8,128)} %concatenate.18, pred[1028]{0:T(1024)(128)(4,1)S(1)} %fusion.89, ...), kind=kLoop, calls=%fused_computation.6 | loop fusion | flops 21748368 | bytes 46680968 | tf_op jit(solution)/shard_map/jit(_where)/select_n | solution.py:116
  144.9 7.3 %fusion.3 = f32[514,1026]{1,0:T(8,128)} fusion(f32[516,1028]{1,0:T(8,128)S(1)} %and_select_fusion, f32[3,518,1030]{2,1,0:T(8,128)} %concatenate.18), kind=kLoop, calls=%fused_computation.12 | loop fusion | flops 3164184 | bytes 14766192 | tf_op jit(solution)/shard_map/mul | solution.py:91
  152.2 28.3 %fusion.27 = f32[512,1024]{1,0:T(8,128)} fusion(f32[514,1026]{1,0:T(8,128)} %get-tuple-element.8, f32[512,1024]{1,0:T(8,128)} %param.11, f32[514,1026]{1,0:T(8,128)} %fusion.3, f32[516,1028]{1,0:T(8,128)} %copy-done.2, f32[514,1026]{1,0:T(8,128)} %get-tuple-element.7), kind=kLoop, calls=%fused_computation.67 | loop fusion | flops 19922944 | bytes 46137344 | tf_op jit(solution)/shard_map/add | solution.py:114
  (78 shorter events, 19.5 us)
Async XLA Ops:
  0.0 20.7 %copy-start = (f32[32,128,128]{2,1,0:T(8,128)S(1)}, f32[32,128,128]{2,1,0:T(8,128)}, u32[]{:S(2)}) copy-start(f32[32,128,128]{2,1,0:T(8,128)} %param.6) | copy-start | bytes 6291460
  1.4 11.6 %all-to-all-start = ((s32[16,2,4]{2,1,0:T(2,128)}), s32[16,2,4]{2,1,0:T(2,128)S(1)}, u32[]{:S(2)}, u32[]{:S(2)}) async-start(s32[16,2,4]{2,1,0:T(2,128)} %broadcast_in_dim.16), calls=%async_computation | async-start | bytes 32768 | tf_op jit(solution)/shard_map/all_to_all | solution.py:20
  15.6 9.8 %all-to-all-start.2 = ((f32[16,1,2]{2,1,0:T(1,128)}), f32[16,1,2]{2,1,0:T(1,128)S(1)}, u32[]{:S(2)}, u32[]{:S(2)}) async-start(f32[16,1,2]{2,1,0:T(1,128)} %bitcast.14), calls=%async_computation.2 | async-start | bytes 16384 | tf_op jit(solution)/shard_map/all_to_all | solution.py:152
  25.3 59.6 %all-to-all-start.1 = ((f32[16,2,128,128]{3,2,1,0:T(8,128)}), f32[16,2,128,128]{3,2,1,0:T(8,128)}, u32[]{:S(2)}, u32[]{:S(2)}) async-start(f32[16,2,128,128]{3,2,1,0:T(8,128)} %bitcast.69), calls=%async_computation.1 | async-start | bytes 4194304 | tf_op jit(solution)/shard_map/all_to_all | solution.py:145
  34.3 1.6 copy-start.10
  34.3 2.2 %copy-start.11 = (f32[512,1024]{1,0:T(8,128)S(1)}, f32[512,1024]{1,0:T(8,128)}, u32[]{:S(2)}) copy-start(f32[512,1024]{1,0:T(8,128)} %param.10) | copy-start | bytes 6291460
  36.5 1.6 copy-start.6
  37.6 1.3 copy-start.7
  37.6 2.0 %copy-start.8 = (f32[1,512,1024]{2,1,0:T(8,128)}, f32[1,512,1024]{2,1,0:T(8,128)S(1)}, u32[]{:S(2)}) copy-start(f32[1,512,1024]{2,1,0:T(8,128)S(1)} %get-tuple-element.20) | copy-start | bytes 6291460
  39.6 15.8 %collective-permute-start.4 = (f32[3,3,1024]{2,1,0:T(4,128)S(1)}, f32[3,3,1024]{2,1,0:T(4,128)S(1)}, u32[]{:S(2)}, u32[]{:S(2)}) collective-permute-start(f32[3,3,1024]{2,1,0:T(4,128)S(1)} %get-tuple-element.13), channel_id=1, source_target_pairs={{0,8},{8,16},{16,24},{24,32},{32,40},{40,48},{48,56},{56,64},{64,7... | collective-permute-start | bytes 110600 | tf_op jit(solution)/shard_map/ppermute | solution.py:37
  42.7 13.2 %collective-permute-start.5 = (f32[3,3,1024]{2,1,0:T(4,128)S(1)}, f32[3,3,1024]{2,1,0:T(4,128)S(1)}, u32[]{:S(2)}, u32[]{:S(2)}) collective-permute-start(f32[3,3,1024]{2,1,0:T(4,128)S(1)} %get-tuple-element.14), channel_id=1, source_target_pairs={{8,0},{16,8},{24,16},{32,24},{40,32},{48,40},{56,48},{64,56},{72,6... | collective-permute-start | bytes 110600 | tf_op jit(solution)/shard_map/ppermute | solution.py:39
  58.6 2.8 %copy-start.5 = (f32[3,518,1024]{2,1,0:T(8,128)}, f32[3,518,1024]{2,1,0:T(8,128)S(1)}, u32[]{:S(2)}) copy-start(f32[3,518,1024]{2,1,0:T(8,128)S(1)} %pad_maximum_fusion) | copy-start | bytes 19095556
  62.0 10.5 %collective-permute-start.6 = (f32[3,518,3]{1,2,0:T(4,128)S(1)}, f32[3,518,3]{1,2,0:T(4,128)S(1)}, u32[]{:S(2)}, u32[]{:S(2)}) collective-permute-start(f32[3,518,3]{1,2,0:T(4,128)S(1)} %copy.77), channel_id=1, source_target_pairs={{0,1},{1,2},{2,3},{3,4},{4,5},{5,6},{6,7},{8,9},{9,10},{10,11},{11... | collective-permute-start | bytes 55952 | tf_op jit(solution)/shard_map/ppermute | solution.py:37
  70.4 5.2 %collective-permute-start.7 = (f32[3,518,3]{1,2,0:T(4,128)S(1)}, f32[3,518,3]{1,2,0:T(4,128)S(1)}, u32[]{:S(2)}, u32[]{:S(2)}) collective-permute-start(f32[3,518,3]{1,2,0:T(4,128)S(1)} %copy.78), channel_id=1, source_target_pairs={{1,0},{2,1},{3,2},{4,3},{5,4},{6,5},{7,6},{9,8},{10,9},{11,10},{12... | collective-permute-start | bytes 55952 | tf_op jit(solution)/shard_map/ppermute | solution.py:39
  99.6 12.5 %collective-permute-start = (f32[4,1024]{1,0:T(4,128)S(1)}, f32[4,1024]{1,0:T(4,128)S(1)}, u32[]{:S(2)}, u32[]{:S(2)}) collective-permute-start(f32[4,1024]{1,0:T(4,128)S(1)} %get-tuple-element.17), channel_id=1, source_target_pairs={{0,8},{8,16},{16,24},{24,32},{32,40},{40,48},{48,56},{56,64},{64,7... | collective-permute-start | bytes 49160 | tf_op jit(solution)/shard_map/ppermute | solution.py:37
  101.5 17.0 %slice-start = ((s8[7188480]{0:T(1024)(128)(4,1)}), s8[4194304]{0:T(1024)(128)(4,1)S(1)}, s32[]{:S(2)}) async-start(s8[7188480]{0:T(1024)(128)(4,1)} %bitcast.64), calls=%async_computation.3 | async-start | bytes 8388608
  101.5 17.0 %slice-start.1 = ((s8[7188480]{0:T(1024)(128)(4,1)}), s8[2994176]{0:T(1024)(128)(4,1)S(1)}, s32[]{:S(2)}) async-start(s8[7188480]{0:T(1024)(128)(4,1)} %bitcast.64), calls=%async_computation.4 | async-start | bytes 5988352
  101.5 10.6 %collective-permute-start.1 = (f32[4,1024]{1,0:T(4,128)S(1)}, f32[4,1024]{1,0:T(4,128)S(1)}, u32[]{:S(2)}, u32[]{:S(2)}) collective-permute-start(f32[4,1024]{1,0:T(4,128)S(1)} %get-tuple-element.18), channel_id=1, source_target_pairs={{8,0},{16,8},{24,16},{32,24},{40,32},{48,40},{56,48},{64,56},{72,6... | collective-permute-start | bytes 49160 | tf_op jit(solution)/shard_map/ppermute | solution.py:39
  112.4 1.4 copy-start.9
  113.9 8.7 %collective-permute-start.2 = (f32[520,4]{1,0:T(8,128)S(1)}, f32[520,4]{1,0:T(8,128)S(1)}, u32[]{:S(2)}, u32[]{:S(2)}) collective-permute-start(f32[520,4]{1,0:T(8,128)S(1)} %get-tuple-element.16), channel_id=1, source_target_pairs={{0,1},{1,2},{2,3},{3,4},{4,5},{5,6},{6,7},{8,9},{9,10},{10,11},{11... | collective-permute-start | bytes 24968 | tf_op jit(solution)/shard_map/ppermute | solution.py:37
  116.3 7.7 %collective-permute-start.3 = (f32[520,4]{1,0:T(8,128)S(1)}, f32[520,4]{1,0:T(8,128)S(1)}, u32[]{:S(2)}, u32[]{:S(2)}) collective-permute-start(f32[520,4]{1,0:T(8,128)S(1)} %get-tuple-element.15), channel_id=1, source_target_pairs={{1,0},{2,1},{3,2},{4,3},{5,4},{6,5},{7,6},{9,8},{10,9},{11,10},{12... | collective-permute-start | bytes 24968 | tf_op jit(solution)/shard_map/ppermute | solution.py:39
  127.2 4.4 %copy-start.3 = (f32[518,1030]{1,0:T(8,128)S(1)}, f32[518,1030]{1,0:T(8,128)}, u32[]{:S(2)}) copy-start(f32[518,1030]{1,0:T(8,128)} %get-tuple-element.9) | copy-start | bytes 6402484
  127.2 4.4 %copy-start.4 = (f32[518,1030]{1,0:T(8,128)S(1)}, f32[518,1030]{1,0:T(8,128)}, u32[]{:S(2)}) copy-start(f32[518,1030]{1,0:T(8,128)} %get-tuple-element.10) | copy-start | bytes 6402484
  144.9 7.3 %copy-start.2 = (f32[516,1028]{1,0:T(8,128)}, f32[516,1028]{1,0:T(8,128)S(1)}, u32[]{:S(2)}) copy-start(f32[516,1028]{1,0:T(8,128)S(1)} %and_select_fusion) | copy-start | bytes 6365380
  152.2 28.3 %copy-start.1 = (f32[32,128,128]{2,1,0:T(8,128)S(1)}, f32[32,128,128]{2,1,0:T(8,128)}, u32[]{:S(2)}) copy-start(f32[32,128,128]{2,1,0:T(8,128)} %param.6) | copy-start | bytes 6291460
where the time goes:
time: 182 us; the launch traced here: 181 us
  other arithmetic  58.6 us (32%)
  starting transfers between devices  47.9 us (26%)
  local copies, waits for them, and re-layouts  46.8 us (26%)
  waiting for transfers between devices  20.5 us (11%)
  matrix products  6.28 us (3%)
    add x1, other arithmetic, relax(): return center + OMEGA * remainder / diagonal  28.3 us
    ppermute x4, starting transfers between devices, padded_2(): lax.ppermute(tail, axis, [(i, (i + 1) % count) for i in range(ends)])  15.5 us
    ppermute x4, starting transfers between devices, padded_2(): lax.ppermute(head, axis, [((i + 1) % count, i) for i in range(ends)])  14.3 us
    select_n x1, other arithmetic, relax(): return jnp.where(inside, center + OMEGA * remainder / safe_diag, 0.0)  13.3 us
    concatenate x2, local copies, waits for them, and re-layouts, padded_2(): jnp.concatenate([lax.ppermute(tail, axis, [(i, (i + 1) % count) for i in...  12.2 us
    mul x2, other arithmetic, relax(): moment = bend_pad * laplace  11.7 us
    squeeze x2, local copies, waits for them, and re-layouts, local(): coeffs[0, coef_cut:full_rows - coef_cut, coef_cut:full_cols - coef_cut]  8.87 us
    ppermute x4, waiting for transfers between devices, padded_2(): lax.ppermute(tail, axis, [(i, (i + 1) % count) for i in range(ends)])  8.44 us
  transfers between devices with their start and end apart: 11, of which 6 were waited for; matrix products, arithmetic and copies ran while one was open for 16% of the time, Pallas kernels for 0%

commit v1 on v0

v1 whole, which is shorter than its diff:
```python
import functools

import jax
import jax.numpy as jnp
from jax import lax
from jax.experimental import pallas as pl
from jax.experimental.pallas import tpu as pltpu
from jax.sharding import PartitionSpec as P

SWEEPS = 2
OMEGA = 0.5
BS = 128
TOP = 16
F32 = jnp.float32
VMEM = pl.BlockSpec(memory_space=pltpu.VMEM)
SMEM = pl.BlockSpec(memory_space=pltpu.SMEM)
ANY = pl.BlockSpec(memory_space=pl.ANY)
HBM = pl.BlockSpec(memory_space=pltpu.HBM)


def lanes():
    return lax.broadcasted_iota(jnp.int32, (8, BS), 1)


def subs():
    return lax.broadcasted_iota(jnp.int32, (8, BS), 0)


def slot_of(owners, position):
    hit = jnp.int32(0)
    for earlier in range(position):
        hit = hit | (owners[earlier] == owners[position]).astype(jnp.int32)
    return hit


def send_kernel(dims, table, field, out, strip, sems, strip_sem):
    ranks, groups, per_device, segments = dims
    me = lax.axis_index("wide")
    first, last, wanted = [], [], []
    for w in range(ranks):
        low, high, any_hit = jnp.int32(0), jnp.int32(0), jnp.int32(0)
        for g in range(groups):
            source = table[w, g]
            local = lax.rem(source, per_device)
            hit = lax.div(source, per_device * segments) == me
            high = jnp.where(hit, local, high)
            any_hit = jnp.where(hit, 1, any_hit)
        for g in reversed(range(groups)):
            source = table[w, g]
            local = lax.rem(source, per_device)
            hit = lax.div(source, per_device * segments) == me
            low = jnp.where(hit, local, low)
        first.append(low)
        last.append(high)
        wanted.append(any_hit)

        @pl.when(any_hit == 1)
        def _():
            for slot, local in ((0, low), (1, high)):
                pltpu.make_async_copy(
                    field.at[local], out.at[w, pl.ds(slot * BS, BS), :], sems.at[w, slot]
                ).start()

    sub = subs()
    for w in range(ranks):
        up, down = max(w - 1, 0), min(w + 1, ranks - 1)
        strip[w, 0:8, :] = jnp.where(
            sub < 4,
            pltpu.roll(field[first[up], BS - 8 : BS, :], 4, 0),
            field[last[up], BS - 8 : BS, :],
        )
        strip[w, 8:16, :] = jnp.where(
            sub < 4,
            field[first[down], 0:8, :],
            pltpu.roll(field[last[down], 0:8, :], 4, 0),
        )
    copy = pltpu.make_async_copy(strip, out.at[:, 2 * BS : 2 * BS + 16, :], strip_sem)
    copy.start()
    for w in range(ranks):

        @pl.when(wanted[w] == 1)
        def _():
            for slot in range(2):
                pltpu.make_async_copy(
                    field.at[0], out.at[w, pl.ds(slot * BS, BS), :], sems.at[w, slot]
                ).wait()

    copy.wait()


def take_kernel(dims, table, recv, left, middle, right, tiles, sems, tile_sems):
    ranks, groups, per_device, segments = dims
    gy_count = groups // 2
    me = lax.axis_index("wide")
    up, down = jnp.maximum(me - 1, 0), jnp.minimum(me + 1, ranks - 1)

    def owners_of(row):
        return [lax.div(table[row, g], per_device * segments) for g in range(groups)]

    mine, above, below = owners_of(me), owners_of(up), owners_of(down)

    def column(gy):
        if gy == 0:
            return left
        if gy == gy_count - 1:
            return right
        return middle.at[gy - 1]

    copies = []
    for gx in range(2):
        for gy in range(gy_count):
            g = gx * gy_count + gy
            start = pl.multiple_of(slot_of(mine, g) * BS, BS)
            copies.append(
                pltpu.make_async_copy(
                    recv.at[mine[g], pl.ds(start, BS), :],
                    column(gy).at[8 + gx * BS : 8 + (gx + 1) * BS, :],
                    sems.at[g],
                )
            )
    for gy in range(gy_count):
        copies.append(
            pltpu.make_async_copy(
                recv.at[above[gy_count + gy], 2 * BS : 2 * BS + 8, :],
                tiles.at[gy],
                tile_sems.at[gy],
            )
        )
        copies.append(
            pltpu.make_async_copy(
                recv.at[below[gy], 2 * BS + 8 : 2 * BS + 16, :],
                tiles.at[gy_count + gy],
                tile_sems.at[gy_count + gy],
            )
        )
    for copy in copies:
        copy.start()
    for copy in copies:
        copy.wait()
    for gy in range(gy_count):
        tile = tiles[gy]
        tile = jnp.where(slot_of(above, gy_count + gy) == 0, pltpu.roll(tile, 4, 0), tile)
        column(gy)[0:8, :] = jnp.where(me > 0, tile, 0.0)
        tile = tiles[gy_count + gy]
        tile = jnp.where(slot_of(below, gy) == 1, pltpu.roll(tile, 4, 0), tile)
        column(gy)[8 + 2 * BS : 16 + 2 * BS, :] = jnp.where(me < ranks - 1, tile, 0.0)


def scale_kernel(dims, table, a_in, b_in, l_in, above, below, a_out, b_out, l_out, to_left, to_right):
    ranks, groups, per_device, segments = dims
    gy_count = groups // 2
    planes = 2 * gy_count
    me = lax.axis_index("wide")
    rows = a_in.shape[0]

    def spacing(row, g):
        source = table[row, g]
        level = table[lax.div(source, per_device * segments), groups + lax.rem(source, per_device)]
        return jnp.where(level >= 1, F32(4.0), F32(1.0))

    lane = lanes()

    def put(row, c, a, b, l):
        a_out[c, pl.ds(row, 8), :] = a
        b_out[c, pl.ds(row, 8), :] = b
        l_out[c, pl.ds(row, 8), :] = l
        if c == 0:
            to_left[pl.ds(row, 8), :] = jnp.where(
                lane < 3,
                a,
                jnp.where(lane < 6, pltpu.roll(b, 3, 1), pltpu.roll(l, 6, 1)),
            )
        if c == planes - 1:
            to_right[pl.ds(row, 8), :] = jnp.where(
                lane >= BS - 3,
                a,
                jnp.where(lane >= BS - 6, pltpu.roll(b, BS - 3, 1), pltpu.roll(l, BS - 6, 1)),
            )

    up, down = jnp.maximum(me - 1, 0), jnp.minimum(me + 1, ranks - 1)
    half = rows // 2
    for gx in range(2):
        factors = [spacing(me, gx * gy_count + gy) for gy in range(gy_count)]

        def step(k, carry):
            row = pl.multiple_of(gx * half + k * 8, 8)
            for c in range(planes):
                s = factors[c // 2]
                cols = slice(c * BS, (c + 1) * BS)
                put(
                    pl.multiple_of(row + TOP, 8),
                    c,
                    a_in[pl.ds(row, 8), cols] * s,
                    b_in[pl.ds(row, 8), cols] * (s * s),
                    l_in[pl.ds(row, 8), cols],
                )
            return carry

        lax.fori_loop(0, half // 8, step, 0)
    for c in range(planes):
        cols = slice(c * BS, (c + 1) * BS)
        s = spacing(up, gy_count + c // 2)
        tile = above[:, cols]
        put(TOP - 8, c, pltpu.roll(tile, 5, 0) * s, pltpu.roll(tile, 2, 0) * (s * s), tile)
        s = spacing(down, c // 2)
        tile = below[:, cols]
        put(TOP + rows, c, tile * s, pltpu.roll(tile, 5, 0) * (s * s), pltpu.roll(tile, 2, 0))


def coef_kernel(dims, a, b, l, from_right, from_left, b8, l8, fx, fy, wt, a8):
    ranks, groups, per_device, segments = dims
    planes = groups
    me, seg = lax.axis_index("wide"), lax.axis_index("narrow")
    rows = a.shape[1] - 2 * TOP
    lane, sub = lanes(), subs()
    strips = rows // 8 + 2

    def side(k, carry):
        row = pl.multiple_of(TOP - 8 + 8 * k, 8)
        z = jnp.where(lane < BS // 2, from_right[pl.ds(row, 8), :], from_left[pl.ds(row, 8), :])
        near = lane < BS // 2
        a8[pl.ds(row, 8), :] = z
        b8[pl.ds(row, 8), :] = jnp.where(near, pltpu.roll(z, BS - 3, 1), pltpu.roll(z, 3, 1))
        l8[pl.ds(row, 8), :] = jnp.where(near, pltpu.roll(z, BS - 6, 1), pltpu.roll(z, 6, 1))
        return carry

    lax.fori_loop(0, strips, side, 0, unroll=2)
    side_ok = ((lane < 2) & (seg < segments - 1)) | ((lane >= BS - 2) & (seg > 0))

    def plane(ref, ref8, c, start):
        return ref8[pl.ds(start, 8), :] if c == planes else ref[c, pl.ds(start, 8), :]

    def step(k, carry):
        row = pl.multiple_of(TOP - 8 + 8 * k, 8)
        at = [plane(a, a8, c, row) for c in range(planes + 1)]
        bt = [plane(b, b8, c, row) for c in range(planes + 1)]
        at_r = [pltpu.roll(t, BS - 1, 1) for t in at]
        bt_r = [pltpu.roll(t, BS - 1, 1) for t in bt]
        bt_l = [pltpu.roll(t, 1, 1) for t in bt]
        face = []
        for c in range(planes + 1):
            nxt = (c + 1) % (planes + 1)
            face.append(0.5 * (at[c] + jnp.where(lane == BS - 1, at_r[nxt], at_r[c])))
        face_l = [pltpu.roll(t, 1, 1) for t in face]
        here = row + sub
        row_ok = ((here >= TOP) | (me > 0)) & ((here < TOP + rows) | (me < ranks - 1))
        for c in range(planes + 1):
            nxt, prv = (c + 1) % (planes + 1), (c + planes) % (planes + 1)
            below = 0.5 * (at[c] + plane(a, a8, c, row + 1))
            above = 0.5 * (at[c] + plane(a, a8, c, row - 1))
            near_b = (
                plane(b, b8, c, row + 1)
                + plane(b, b8, c, row - 1)
                + jnp.where(lane == BS - 1, bt_r[nxt], bt_r[c])
                + jnp.where(lane == 0, bt_l[prv], bt_l[c])
            )
            diag = (
                16.0 * bt[c]
                + face[c]
                + jnp.where(lane == 0, face_l[prv], face_l[c])
                + below
                + above
                + near_b
            )
            ok = row_ok & side_ok if c == planes else row_ok
            fx[c, pl.ds(row, 8), :] = face[c]
            fy[c, pl.ds(row, 8), :] = below
            wt[c, pl.ds(row, 8), :] = jnp.where(ok, OMEGA / jnp.where(ok, diag, 1.0), 0.0)
        return carry

    lax.fori_loop(0, strips, step, 0)


def split3(x):
    high = x.astype(jnp.bfloat16)
    rest = x - high.astype(F32)
    mid = rest.astype(jnp.bfloat16)
    low = (rest - mid.astype(F32)).astype(jnp.bfloat16)
    return jnp.concatenate([high, mid, low], axis=1)


def refine_rows(src, put, strips):
    sub = subs()

    def step(k, carry):
        row = pl.multiple_of(8 * k, 8)
        x = src[pl.ds(row + 8, 8), :]
        up = src[pl.ds(row + 7, 8), :]
        down = src[pl.ds(row + 9, 8), :]
        part = lax.rem(k, 8)
        up = jnp.where((sub == 0) & (part == 1), x, up)
        down = jnp.where((sub == 7) & (part == 0), x, down)
        near = 0.75 * x
        put(row, near + 0.25 * up, near + 0.25 * down)
        return carry

    lax.fori_loop(0, strips, step, 0, unroll=2)


def refine_kernel(weights, left, middle, right, v, cols):
    gy_count = v.shape[0] // 2
    strips = left.shape[0] // 8
    for gy in range(gy_count):
        parent = left[...] if gy == 0 else right[...] if gy == gy_count - 1 else middle[gy - 1]
        wide = jnp.dot(split3(parent), weights[...], preferred_element_type=F32)
        for half in range(2):
            cols[gy, half, 8 : 8 + left.shape[0], :] = wide[:, half * BS : (half + 1) * BS]

            def put(row, even, odd, c=2 * gy + half):
                v[c, pl.ds(2 * row, 8, stride=2), :] = even
                v[c, pl.ds(2 * row + 1, 8, stride=2), :] = odd

            refine_rows(cols.at[gy, half], put, strips)


def sweep_kernel(weights, from_right, from_left, v, b, l, b8, l8, fx, fy, wt, out, v8, cols, m, h, v1):
    planes = v.shape[0]
    rows = out.shape[0]
    lane = lanes()
    cells = from_right.shape[0]
    wide_lane = lax.broadcasted_iota(jnp.int32, (cells, BS), 1)
    edge = jnp.where(wide_lane < BS // 2, from_right[...], from_left[...])
    cols[8 : 8 + cells, :] = jnp.dot(split3(edge), weights[...], preferred_element_type=F32)

    def put(row, even, odd):
        v8[pl.ds(2 * row, 8, stride=2), :] = even
        v8[pl.ds(2 * row + 1, 8, stride=2), :] = odd

    refine_rows(cols, put, cells // 8)

    def plane(ref, ref8, c, start):
        return ref8[pl.ds(start, 8), :] if c == planes else ref[c, pl.ds(start, 8), :]

    def right_of(ts):
        r = [pltpu.roll(t, BS - 1, 1) for t in ts]
        n = len(ts)
        return [jnp.where(lane == BS - 1, r[(c + 1) % n], r[c]) for c in range(n)]

    def left_of(ts):
        r = [pltpu.roll(t, 1, 1) for t in ts]
        n = len(ts)
        return [jnp.where(lane == 0, r[(c + n - 1) % n], r[c]) for c in range(n)]

    def moments(get):
        def step(k, carry):
            row = pl.multiple_of(TOP - 8 + 8 * k, 8)
            t = [get(c, row) for c in range(planes + 1)]
            dx = [r - x for r, x in zip(right_of(t), t)]
            q = [fx[c, pl.ds(row, 8), :] * dx[c] for c in range(planes + 1)]
            dxl, ql = left_of(dx), left_of(q)
            for c in range(planes + 1):
                dyd = get(c, row + 1) - t[c]
                dyu = t[c] - get(c, row - 1)
                lap = (dx[c] - dxl[c]) + (dyd - dyu)
                m[c, pl.ds(row, 8), :] = plane(b, b8, c, row) * lap
                div = (q[c] - ql[c]) + (
                    fy[c, pl.ds(row, 8), :] * dyd - fy[c, pl.ds(row - 1, 8), :] * dyu
                )
                h[c, pl.ds(row, 8), :] = plane(l, l8, c, row) + div
            return carry

        lax.fori_loop(0, rows // 8 + 2, step, 0, unroll=2)

    def update(first, count, get, put, width):
        def step(k, carry):
            row = pl.multiple_of(first + 8 * k, 8)
            t = [m[c, pl.ds(row, 8), :] for c in range(planes + 1)]
            tr, tl = right_of(t), left_of(t)
            for c in range(width):
                lap = (
                    tr[c] + tl[c] + m[c, pl.ds(row - 1, 8), :] + m[c, pl.ds(row + 1, 8), :]
                ) - 4.0 * t[c]
                put(c, row, get(c, row) + wt[c, pl.ds(row, 8), :] * (h[c, pl.ds(row, 8), :] - lap))
            return carry

        lax.fori_loop(0, count, step, 0, unroll=2)

    def start_value(c, row):
        return plane(v, v8, c, row)

    def put_middle(c, row, value):
        v1[c, pl.ds(row, 8), :] = value

    def middle_value(c, row):
        return v1[c, pl.ds(row, 8), :]

    def put_out(c, row, value):
        out[pl.ds(pl.multiple_of(row - TOP, 8), 8), c * BS : (c + 1) * BS] = value

    moments(start_value)
    update(TOP - 8, rows // 8 + 2, start_value, put_middle, planes + 1)
    moments(middle_value)
    update(TOP, rows // 8, middle_value, put_out, planes)


def quadrant_table(half_index):
    half_size = BS // 2
    row_ids = jnp.arange(BS, dtype=jnp.int32)[:, None]
    col_ids = jnp.arange(BS, dtype=jnp.int32)[None, :]
    base_cell = half_index * half_size
    near_cell = base_cell + row_ids // 2
    other_cell = near_cell + jnp.where(row_ids % 2 == 1, 1, -1)
    other_cell = jnp.clip(other_cell, base_cell, base_cell + half_size - 1)
    return 0.75 * (col_ids == near_cell).astype(F32) + 0.25 * (col_ids == other_cell).astype(F32)


def params(limit_mib):
    return pltpu.CompilerParams(vmem_limit_bytes=limit_mib << 20)


def shape(*dims):
    return jax.ShapeDtypeStruct(dims, F32)


def local(old_field, old_level, new_source, stretch_coef, bend_coef, load_field):
    per_device = old_field.shape[0]
    groups_x, groups_y = new_source.shape
    groups = groups_x * groups_y
    ranks, segments = lax.axis_size("wide"), lax.axis_size("narrow")
    dims = (ranks, groups, per_device, segments)
    rows, columns = load_field.shape
    planes = columns // BS
    tall = rows + 2 * TOP
    coarse = 2 * BS + 16
    up_links = [(i + 1, i) for i in range(ranks - 1)]
    down_links = [(i, i + 1) for i in range(ranks - 1)]
    left_links = [(i + 1, i) for i in range(segments - 1)]
    right_links = [(i, i + 1) for i in range(segments - 1)]

    facts = jnp.concatenate([new_source.reshape(-1), old_level])
    table = lax.all_to_all(
        jnp.broadcast_to(facts[None], (ranks, groups + per_device)), "wide", 0, 0, tiled=True
    )

    head = jnp.concatenate([stretch_coef[:3], bend_coef[:3], load_field[:2]])
    tail = jnp.concatenate([stretch_coef[-3:], bend_coef[-3:], load_field[-2:]])
    above = lax.ppermute(tail, "wide", down_links)
    below = lax.ppermute(head, "wide", up_links)

    table, above, below = lax.optimization_barrier((table, above, below))
    outgoing = pl.pallas_call(
        functools.partial(send_kernel, dims),
        out_shape=shape(ranks, coarse, BS),
        in_specs=[SMEM, VMEM],
        out_specs=HBM,
        scratch_shapes=[
            pltpu.VMEM((ranks, 16, BS), F32),
            pltpu.SemaphoreType.DMA((ranks, 2)),
            pltpu.SemaphoreType.DMA(()),
        ],
        compiler_params=params(8),
        name="send_build",
    )(table, old_field)
    incoming = lax.all_to_all(outgoing, "wide", 0, 0, tiled=True)

    a, b, l, to_left, to_right = pl.pallas_call(
        functools.partial(scale_kernel, dims),
        out_shape=[shape(planes, tall, BS)] * 3 + [shape(tall, BS)] * 2,
        in_specs=[SMEM] + [VMEM] * 5,
        out_specs=[VMEM] * 5,
        compiler_params=params(20),
        name="scale",
    )(table, stretch_coef, bend_coef, load_field, above, below)
    from_right = lax.ppermute(to_left, "narrow", left_links)
    from_left = lax.ppermute(to_right, "narrow", right_links)
    b8, l8, fx, fy, wt = pl.pallas_call(
        functools.partial(coef_kernel, dims),
        out_shape=[shape(tall, BS)] * 2 + [shape(planes + 1, tall, BS)] * 3,
        in_specs=[VMEM] * 5,
        out_specs=[VMEM] * 5,
        scratch_shapes=[pltpu.VMEM((tall, BS), F32)],
        compiler_params=params(24),
        name="coef",
    )(a, b, l, from_right, from_left)

    incoming, b8, l8, fx, fy, wt = lax.optimization_barrier((incoming, b8, l8, fx, fy, wt))

    left, middle, right = pl.pallas_call(
        functools.partial(take_kernel, dims),
        out_shape=[shape(coarse, BS), shape(groups_y - 2, coarse, BS), shape(coarse, BS)],
        in_specs=[SMEM, ANY],
        out_specs=[VMEM] * 3,
        scratch_shapes=[
            pltpu.VMEM((2 * groups_y, 8, BS), F32),
            pltpu.SemaphoreType.DMA((groups,)),
            pltpu.SemaphoreType.DMA((2 * groups_y,)),
        ],
        compiler_params=params(4),
        name="take",
    )(table, incoming)
    edge_right = lax.ppermute(left, "narrow", left_links)
    edge_left = lax.ppermute(right, "narrow", right_links)

    low, high = quadrant_table(0).T, quadrant_table(1).T
    both = jnp.concatenate([low, high], axis=1).astype(jnp.bfloat16)
    rim = jnp.concatenate([low[:, : BS // 2], high[:, BS // 2 :]], axis=1).astype(jnp.bfloat16)
    v = pl.pallas_call(
        refine_kernel,
        out_shape=shape(planes, tall, BS),
        in_specs=[VMEM] * 4,
        out_specs=VMEM,
        scratch_shapes=[pltpu.VMEM((groups_y, 2, coarse + 16, BS), F32)],
        compiler_params=params(12),
        name="refine",
    )(jnp.concatenate([both] * 3), left, middle, right)
    return pl.pallas_call(
        sweep_kernel,
        out_shape=shape(rows, columns),
        in_specs=[VMEM] * 11,
        out_specs=VMEM,
        scratch_shapes=[
            pltpu.VMEM((tall, BS), F32),
            pltpu.VMEM((coarse + 16, BS), F32),
            pltpu.VMEM((planes + 1, tall, BS), F32),
            pltpu.VMEM((planes + 1, tall, BS), F32),
            pltpu.VMEM((planes + 1, tall, BS), F32),
        ],
        compiler_params=params(32),
        name="sweeps",
    )(jnp.concatenate([rim] * 3), edge_right, edge_left, v, b, l, b8, l8, fx, fy, wt)


def solution(mesh):
    return jax.shard_map(
        local,
        mesh=mesh,
        in_specs=(
            P(("wide", "narrow"), None, None),
            P(("wide", "narrow")),
            P("wide", "narrow"),
            P("wide", "narrow"),
            P("wide", "narrow"),
            P("wide", "narrow"),
        ),
        out_specs=P("wide", "narrow"),
        check_vma=False,
    )
```

time: 182 us -> 114 us (0.63)
  other arithmetic: 58.6 us -> 0.94 us
  Pallas kernels: 0 us -> 48.6 us
  local copies, waits for them, and re-layouts: 46.8 us -> 22.5 us
  starting transfers between devices: 47.9 us -> 27.9 us
  waiting for transfers between devices: 20.5 us -> 3.36 us
  blocking collectives: 0 us -> 9.28 us
  matrix products: 6.28 us -> 0 us
    pallas_call x0 -> x6, Pallas kernels: none -> 48.6 us  [the longest x1 22 us: local(): pl.pallas_call(sweep_kernel, out_shape=shape(rows, columns), in_specs=[VM...]
    add x3 -> x0, other arithmetic: 28.5 us -> none  [the longest x1 28.3 us: relax(): return center + OMEGA * remainder / diagonal]
    select_n x4 -> x0, other arithmetic: 13.3 us -> none  [the longest x1 13.3 us: relax(): return jnp.where(inside, center + OMEGA * remainder / safe_diag, 0.0)]
    all_to_all x3 -> x1, starting transfers between devices: 18 us -> 5.72 us  [local(): incoming = lax.all_to_all(outgoing, 'wide', 0, 0, tiled=True)]
    concatenate x2 -> x0, local copies, waits for them, and re-layouts: 12.2 us -> none  [padded_2(): jnp.concatenate([lax.ppermute(tail, axis, [(i, (i + 1) % count) for i in...]
    unnamed x29 -> x30, local copies, waits for them, and re-layouts: 8.32 us -> 20 us
    mul x2 -> x0, other arithmetic: 11.7 us -> none  [relax(): moment = bend_pad * laplace]
    ppermute x8 -> x6, waiting for transfers between devices: 13.2 us -> 3.36 us  [the longest x1 2.46 us: local(): from_right = lax.ppermute(to_left, 'narrow', left_links)]
  transfers between devices with their start and end apart: 11 -> 7, of which waited for: 6 -> 2; matrix products, arithmetic and copies ran while one was open for 16% -> 2% of each run, Pallas kernels for 0% -> 20%
where the time goes in v1:
time: 114 us; the launch traced here: 113 us
  Pallas kernels  48.6 us (43%)
  starting transfers between devices  27.9 us (24%)
  local copies, waits for them, and re-layouts  22.5 us (20%)
  blocking collectives  9.28 us (8%)
  waiting for transfers between devices  3.36 us (3%)
    pallas_call x1, Pallas kernels, local(): pl.pallas_call(sweep_kernel, out_shape=shape(rows, columns), in_specs=[VM...  22 us
    unnamed x30, local copies, waits for them, and re-layouts  20 us
    pallas_call x1, Pallas kernels, local(): pl.pallas_call(functools.partial(coef_kernel, dims), out_shape=[shape(tal...  13.6 us
    all_to_all x1, blocking collectives, local(): lax.all_to_all(jnp.broadcast_to(facts[None], (ranks, groups + per_device)...  9.28 us
    pallas_call x1, Pallas kernels, local(): pl.pallas_call(functools.partial(scale_kernel, dims), out_shape=[shape(pl...  5.97 us
    all_to_all x1, starting transfers between devices, local(): incoming = lax.all_to_all(outgoing, 'wide', 0, 0, tiled=True)  5.72 us
    ppermute x1, starting transfers between devices, local(): from_right = lax.ppermute(to_left, 'narrow', left_links)  4.69 us
    ppermute x1, starting transfers between devices, local(): edge_left = lax.ppermute(right, 'narrow', right_links)  4.39 us
  transfers between devices with their start and end apart: 7, of which 2 were waited for; matrix products, arithmetic and copies ran while one was open for 2% of the time, Pallas kernels for 20%

profile of v1, /device:TPU:7, one launch (start us, length us, event | category | flops | bytes accessed | tf_op | source)
XLA Modules:
  0.0 112.7 jit_solution(16145691676249841514)
XLA Ops:
  0.0 0.8 fusion.2
  0.8 0.8 fusion
  1.6 3.2 %collective-permute-start = (f32[8,1024]{1,0:T(8,128)S(1)}, f32[8,1024]{1,0:T(8,128)S(1)}, u32[]{:S(2)}, u32[]{:S(2)}) collective-permute-start(f32[8,1024]{1,0:T(8,128)S(1)} %pad_maximum_fusion), channel_id=1, source_target_pairs={{0,8},{8,16},{16,24},{24,32},{32,40},{40,48},{48,56},{56,64},{64,7... | collective-permute-start | bytes 98312 | tf_op jit(solution)/shard_map/ppermute | solution.py:437
  4.9 4.2 %collective-permute-start.1 = (f32[8,1024]{1,0:T(8,128)S(1)}, f32[8,1024]{1,0:T(8,128)S(1)}, u32[]{:S(2)}, u32[]{:S(2)}) collective-permute-start(f32[8,1024]{1,0:T(8,128)S(1)} %pad_maximum_fusion.1), channel_id=1, source_target_pairs={{8,0},{16,8},{24,16},{32,24},{40,32},{48,40},{56,48},{64,56},{72,6... | collective-permute-start | bytes 98312 | tf_op jit(solution)/shard_map/ppermute | solution.py:438
  9.1 0.8 reshape.77
  10.6 9.3 %all_to_all.14 = s32[16,1,40]{2,1,0:T(1,128)S(1)} all-to-all(s32[16,1,40]{2,1,0:T(1,128)S(1)} %broadcast_in_dim.6), channel_id=1, replica_groups=mesh['wide'=16,'narrow'=8] {'wide'}, dimensions={0} | all-to-all | bytes 5120 | tf_op jit(solution)/shard_map/all_to_all | solution.py:431
  19.9 1.6 %copy-done.14 = f32[32,128,128]{2,1,0:T(8,128)S(1)} copy-done((f32[32,128,128]{2,1,0:T(8,128)S(1)}, f32[32,128,128]{2,1,0:T(8,128)}, u32[]{:S(2)}) %copy-start.14) | copy-done | bytes 2097176
  21.4 2.2 %send_build.1 = f32[16,272,128]{2,1,0:T(8,128)S(1)} custom-call(s32[16,40]{1,0:T(8,128)S(1)} %bitcast.2, f32[32,128,128]{2,1,0:T(8,128)S(1)} %copy-done.14), custom_call_target="tpu_custom_call" | custom-call | tf_op jit(solution)/shard_map/send_build/pallas_call | solution.py:441
  23.7 1.3 %copy-done = f32[16,272,128]{2,1,0:T(8,128)} copy-done((f32[16,272,128]{2,1,0:T(8,128)}, f32[16,272,128]{2,1,0:T(8,128)S(1)}, u32[]{:S(2)}) %copy-start) | copy-done | bytes 2228248
  25.0 5.7 %all-to-all-start.1 = ((f32[16,272,128]{2,1,0:T(8,128)}), f32[16,272,128]{2,1,0:T(8,128)S(1)}, u32[]{:S(2)}, u32[]{:S(2)}) async-start(f32[16,272,128]{2,1,0:T(8,128)} %copy-done), calls=%async_computation.1 | async-start | bytes 4456448 | tf_op jit(solution)/shard_map/all_to_all | solution.py:454
  30.8 1.6 %copy-done.11 = f32[512,1024]{1,0:T(8,128)S(1)} copy-done((f32[512,1024]{1,0:T(8,128)S(1)}, f32[512,1024]{1,0:T(8,128)}, u32[]{:S(2)}) %copy-start.11) | copy-done | bytes 2097176
  32.3 1.6 %copy-done.12 = f32[512,1024]{1,0:T(8,128)S(1)} copy-done((f32[512,1024]{1,0:T(8,128)S(1)}, f32[512,1024]{1,0:T(8,128)}, u32[]{:S(2)}) %copy-start.12) | copy-done | bytes 2097176
  33.9 1.6 %copy-done.13 = f32[512,1024]{1,0:T(8,128)S(1)} copy-done((f32[512,1024]{1,0:T(8,128)S(1)}, f32[512,1024]{1,0:T(8,128)}, u32[]{:S(2)}) %copy-start.13) | copy-done | bytes 2097176
  35.5 6.0 %scale.1 = (f32[8,544,128]{2,1,0:T(8,128)S(1)}, f32[8,544,128]{2,1,0:T(8,128)S(1)}, f32[8,544,128]{2,1,0:T(8,128)S(1)}, f32[544,128]{1,0:T(8,128)S(1)}, f32[544,128]{1,0:T(8,128)S(1)}) custom-call(s32[16,40]{1,0:T(8,128)S(1)} %bitcast.3, f32[512,1024]{1,0:T(8,128)S(1)} %copy-done.11, f32[512,1024]{1,0:T(8,128)S(1)} %copy-done.12, ...), custom_call_target="tpu_custom_call" | custom-call | tf_op jit(solution)/shard_map/scale/pallas_call | solution.py:456
  41.5 4.7 %collective-permute-start.2 = (f32[544,128]{1,0:T(8,128)S(1)}, f32[544,128]{1,0:T(8,128)S(1)}, u32[]{:S(2)}, u32[]{:S(2)}) collective-permute-start(f32[544,128]{1,0:T(8,128)S(1)} %get-tuple-element.33), channel_id=1, source_target_pairs={{1,0},{2,1},{3,2},{4,3},{5,4},{6,5},{7,6},{9,8},{10,9},{11,10},{12... | collective-permute-start | bytes 835592 | tf_op jit(solution)/shard_map/ppermute | solution.py:464
  46.2 3.6 %collective-permute-start.3 = (f32[544,128]{1,0:T(8,128)S(1)}, f32[544,128]{1,0:T(8,128)S(1)}, u32[]{:S(2)}, u32[]{:S(2)}) collective-permute-start(f32[544,128]{1,0:T(8,128)S(1)} %get-tuple-element.34), channel_id=1, source_target_pairs={{0,1},{1,2},{2,3},{3,4},{4,5},{5,6},{6,7},{8,9},{9,10},{10,11},{11... | collective-permute-start | bytes 835592 | tf_op jit(solution)/shard_map/ppermute | solution.py:465
  49.9 2.5 %collective-permute-done.2.from_right = f32[544,128]{1,0:T(8,128)S(1)} collective-permute-done((f32[544,128]{1,0:T(8,128)S(1)}, f32[544,128]{1,0:T(8,128)S(1)}, u32[]{:S(2)}, u32[]{:S(2)}) %collective-permute-start.2) | collective-permute-done | bytes 278560 | tf_op jit(solution)/shard_map/ppermute | solution.py:464
  52.4 0.9 collective-permute-done.3.from_left
  53.3 13.6 %coef.1 = (f32[544,128]{1,0:T(8,128)S(1)}, f32[544,128]{1,0:T(8,128)S(1)}, f32[9,544,128]{2,1,0:T(8,128)S(1)}, f32[9,544,128]{2,1,0:T(8,128)S(1)}, f32[9,544,128]{2,1,0:T(8,128)S(1)}) custom-call(f32[8,544,128]{2,1,0:T(8,128)S(1)} %get-tuple-element.30.a, f32[8,544,128]{2,1,0:T(8,128)S(1)} %get-tuple-element.31.b, f32[8,544,128]{2,1,0:T(8,128)S(1)} %get-tuple-element.32.l, ...), custom_call_target="tpu_custom_call" | custom-call | tf_op jit(solution)/shard_map/coef/pallas_call | solution.py:466
  66.9 1.4 %copy-done.1 = f32[8,544,128]{2,1,0:T(8,128)} copy-done((f32[8,544,128]{2,1,0:T(8,128)}, f32[8,544,128]{2,1,0:T(8,128)S(1)}, u32[]{:S(2)}) %copy-start.1) | copy-done | bytes 2228248
  68.3 1.4 %copy-done.3 = f32[8,544,128]{2,1,0:T(8,128)} copy-done((f32[8,544,128]{2,1,0:T(8,128)}, f32[8,544,128]{2,1,0:T(8,128)S(1)}, u32[]{:S(2)}) %copy-start.3) | copy-done | bytes 2228248
  69.7 1.5 %copy-done.5 = f32[9,544,128]{2,1,0:T(8,128)} copy-done((f32[9,544,128]{2,1,0:T(8,128)}, f32[9,544,128]{2,1,0:T(8,128)S(1)}, u32[]{:S(2)}) %copy-start.5) | copy-done | bytes 2506776
  71.2 1.5 %copy-done.7 = f32[9,544,128]{2,1,0:T(8,128)} copy-done((f32[9,544,128]{2,1,0:T(8,128)}, f32[9,544,128]{2,1,0:T(8,128)S(1)}, u32[]{:S(2)}) %copy-start.7) | copy-done | bytes 2506776
  72.7 1.4 %copy-done.9 = f32[9,544,128]{2,1,0:T(8,128)} copy-done((f32[9,544,128]{2,1,0:T(8,128)}, f32[9,544,128]{2,1,0:T(8,128)S(1)}, u32[]{:S(2)}) %copy-start.9) | copy-done | bytes 2506776
  74.1 1.8 %take.1 = (f32[272,128]{1,0:T(8,128)S(1)}, f32[2,272,128]{2,1,0:T(8,128)S(1)}, f32[272,128]{1,0:T(8,128)S(1)}) custom-call(s32[16,40]{1,0:T(8,128)S(1)} %bitcast.4, f32[16,272,128]{2,1,0:T(8,128)S(1)} %all-to-all-done.1.recv), custom_call_target="tpu_custom_call" | custom-call | tf_op jit(solution)/shard_map/take/pallas_call | solution.py:478
  76.0 2.1 %collective-permute-start.4 = (f32[272,128]{1,0:T(8,128)S(1)}, f32[272,128]{1,0:T(8,128)S(1)}, u32[]{:S(2)}, u32[]{:S(2)}) collective-permute-start(f32[272,128]{1,0:T(8,128)S(1)} %get-tuple-element.41.left), channel_id=1, source_target_pairs={{1,0},{2,1},{3,2},{4,3},{5,4},{6,5},{7,6},{9,8},{10,9},{11,10},{12... | collective-permute-start | bytes 417800 | tf_op jit(solution)/shard_map/ppermute | solution.py:491
  78.0 4.4 %collective-permute-start.5 = (f32[272,128]{1,0:T(8,128)S(1)}, f32[272,128]{1,0:T(8,128)S(1)}, u32[]{:S(2)}, u32[]{:S(2)}) collective-permute-start(f32[272,128]{1,0:T(8,128)S(1)} %get-tuple-element.42.right), channel_id=1, source_target_pairs={{0,1},{1,2},{2,3},{3,4},{4,5},{5,6},{6,7},{8,9},{9,10},{10,11},{11... | collective-permute-start | bytes 417800 | tf_op jit(solution)/shard_map/ppermute | solution.py:492
  82.5 3.0 %refine.1.v = f32[8,544,128]{2,1,0:T(8,128)S(1)} custom-call(bf16[384,256]{1,0:T(8,128)(2,1)S(1)} %maximum_maximum_fusion.weights, f32[272,128]{1,0:T(8,128)S(1)} %get-tuple-element.41.left, f32[2,272,128]{2,1,0:T(8,128)S(1)} %get-tuple-element.43.middle, f32[272,128]{1,0:T(8,128)S(1)} %get-tuple-element.42.right), custom_call_target="tpu_custom_call" | custom-call | tf_op jit(solution)/shard_map/refine/pallas_call | solution.py:497
  85.6 1.7 %copy-done.6 = f32[9,544,128]{2,1,0:T(8,128)S(1)} copy-done((f32[9,544,128]{2,1,0:T(8,128)S(1)}, f32[9,544,128]{2,1,0:T(8,128)}, u32[]{:S(2)}) %copy-start.6) | copy-done | bytes 2506776
  87.3 1.7 %copy-done.8 = f32[9,544,128]{2,1,0:T(8,128)S(1)} copy-done((f32[9,544,128]{2,1,0:T(8,128)S(1)}, f32[9,544,128]{2,1,0:T(8,128)}, u32[]{:S(2)}) %copy-start.8) | copy-done | bytes 2506776
  89.0 1.7 %copy-done.10 = f32[9,544,128]{2,1,0:T(8,128)S(1)} copy-done((f32[9,544,128]{2,1,0:T(8,128)S(1)}, f32[9,544,128]{2,1,0:T(8,128)}, u32[]{:S(2)}) %copy-start.10) | copy-done | bytes 2506776
  90.7 22.0 %sweeps.1 = f32[512,1024]{1,0:T(8,128)} custom-call(bf16[384,128]{1,0:T(8,128)(2,1)S(1)} %maximum_maximum_fusion.1.weights, f32[272,128]{1,0:T(8,128)S(1)} %collective-permute-done.4.from_right, f32[272,128]{1,0:T(8,128)S(1)} %collective-permute-done.5.from_left, f32[8,544,128]{2,1,0:T(8,128)S(1)} %refine.1.v, f32[8,544,128]{2,1,0:T(8,128)S(1)} %copy-done.2, ...), custom_call_target="tpu_custom_call" | custom-call | tf_op jit(solution)/shard_map/sweeps/pallas_call | solution.py:506
  (33 shorter events, 1.1 us)
Async XLA Ops:
  1.6 18.2 %collective-permute-start = (f32[8,1024]{1,0:T(8,128)S(1)}, f32[8,1024]{1,0:T(8,128)S(1)}, u32[]{:S(2)}, u32[]{:S(2)}) collective-permute-start(f32[8,1024]{1,0:T(8,128)S(1)} %pad_maximum_fusion), channel_id=1, source_target_pairs={{0,8},{8,16},{16,24},{24,32},{32,40},{40,48},{48,56},{56,64},{64,7... | collective-permute-start | bytes 98312 | tf_op jit(solution)/shard_map/ppermute | solution.py:437
  4.9 15.0 %collective-permute-start.1 = (f32[8,1024]{1,0:T(8,128)S(1)}, f32[8,1024]{1,0:T(8,128)S(1)}, u32[]{:S(2)}, u32[]{:S(2)}) collective-permute-start(f32[8,1024]{1,0:T(8,128)S(1)} %pad_maximum_fusion.1), channel_id=1, source_target_pairs={{8,0},{16,8},{24,16},{32,24},{40,32},{48,40},{56,48},{64,56},{72,6... | collective-permute-start | bytes 98312 | tf_op jit(solution)/shard_map/ppermute | solution.py:438
  19.8 1.6 %copy-start.14 = (f32[32,128,128]{2,1,0:T(8,128)S(1)}, f32[32,128,128]{2,1,0:T(8,128)}, u32[]{:S(2)}) copy-start(f32[32,128,128]{2,1,0:T(8,128)} %field.1) | copy-start | bytes 6291460
  23.7 1.3 %copy-start = (f32[16,272,128]{2,1,0:T(8,128)}, f32[16,272,128]{2,1,0:T(8,128)S(1)}, u32[]{:S(2)}) copy-start(f32[16,272,128]{2,1,0:T(8,128)S(1)} %send_build.1) | copy-start | bytes 6684676
  25.0 49.1 %all-to-all-start.1 = ((f32[16,272,128]{2,1,0:T(8,128)}), f32[16,272,128]{2,1,0:T(8,128)S(1)}, u32[]{:S(2)}, u32[]{:S(2)}) async-start(f32[16,272,128]{2,1,0:T(8,128)} %copy-done), calls=%async_computation.1 | async-start | bytes 4456448 | tf_op jit(solution)/shard_map/all_to_all | solution.py:454
  30.7 1.6 %copy-start.11 = (f32[512,1024]{1,0:T(8,128)S(1)}, f32[512,1024]{1,0:T(8,128)}, u32[]{:S(2)}) copy-start(f32[512,1024]{1,0:T(8,128)} %a_in.1) | copy-start | bytes 6291460
  32.3 1.6 %copy-start.12 = (f32[512,1024]{1,0:T(8,128)S(1)}, f32[512,1024]{1,0:T(8,128)}, u32[]{:S(2)}) copy-start(f32[512,1024]{1,0:T(8,128)} %b_in.1) | copy-start | bytes 6291460
  33.9 1.6 %copy-start.13 = (f32[512,1024]{1,0:T(8,128)S(1)}, f32[512,1024]{1,0:T(8,128)}, u32[]{:S(2)}) copy-start(f32[512,1024]{1,0:T(8,128)} %l_in.1) | copy-start | bytes 6291460
  41.5 10.9 %collective-permute-start.2 = (f32[544,128]{1,0:T(8,128)S(1)}, f32[544,128]{1,0:T(8,128)S(1)}, u32[]{:S(2)}, u32[]{:S(2)}) collective-permute-start(f32[544,128]{1,0:T(8,128)S(1)} %get-tuple-element.33), channel_id=1, source_target_pairs={{1,0},{2,1},{3,2},{4,3},{5,4},{6,5},{7,6},{9,8},{10,9},{11,10},{12... | collective-permute-start | bytes 835592 | tf_op jit(solution)/shard_map/ppermute | solution.py:464
  46.2 7.1 %collective-permute-start.3 = (f32[544,128]{1,0:T(8,128)S(1)}, f32[544,128]{1,0:T(8,128)S(1)}, u32[]{:S(2)}, u32[]{:S(2)}) collective-permute-start(f32[544,128]{1,0:T(8,128)S(1)} %get-tuple-element.34), channel_id=1, source_target_pairs={{0,1},{1,2},{2,3},{3,4},{4,5},{5,6},{6,7},{8,9},{9,10},{10,11},{11... | collective-permute-start | bytes 835592 | tf_op jit(solution)/shard_map/ppermute | solution.py:465
  66.9 1.4 %copy-start.1 = (f32[8,544,128]{2,1,0:T(8,128)}, f32[8,544,128]{2,1,0:T(8,128)S(1)}, u32[]{:S(2)}) copy-start(f32[8,544,128]{2,1,0:T(8,128)S(1)} %get-tuple-element.31.b) | copy-start | bytes 6684676
  68.3 1.4 %copy-start.3 = (f32[8,544,128]{2,1,0:T(8,128)}, f32[8,544,128]{2,1,0:T(8,128)S(1)}, u32[]{:S(2)}) copy-start(f32[8,544,128]{2,1,0:T(8,128)S(1)} %get-tuple-element.32.l) | copy-start | bytes 6684676
  69.7 1.5 %copy-start.5 = (f32[9,544,128]{2,1,0:T(8,128)}, f32[9,544,128]{2,1,0:T(8,128)S(1)}, u32[]{:S(2)}) copy-start(f32[9,544,128]{2,1,0:T(8,128)S(1)} %get-tuple-element.46.fx) | copy-start | bytes 7520260
  71.2 1.5 %copy-start.7 = (f32[9,544,128]{2,1,0:T(8,128)}, f32[9,544,128]{2,1,0:T(8,128)S(1)}, u32[]{:S(2)}) copy-start(f32[9,544,128]{2,1,0:T(8,128)S(1)} %get-tuple-element.47.fy) | copy-start | bytes 7520260
  72.7 1.4 %copy-start.9 = (f32[9,544,128]{2,1,0:T(8,128)}, f32[9,544,128]{2,1,0:T(8,128)S(1)}, u32[]{:S(2)}) copy-start(f32[9,544,128]{2,1,0:T(8,128)S(1)} %get-tuple-element.48.wt) | copy-start | bytes 7520260
  74.1 11.4 %copy-start.4 = (f32[8,544,128]{2,1,0:T(8,128)S(1)}, f32[8,544,128]{2,1,0:T(8,128)}, u32[]{:S(2)}) copy-start(f32[8,544,128]{2,1,0:T(8,128)} %copy-done.3) | copy-start | bytes 6684676
  76.0 9.6 %copy-start.2 = (f32[8,544,128]{2,1,0:T(8,128)S(1)}, f32[8,544,128]{2,1,0:T(8,128)}, u32[]{:S(2)}) copy-start(f32[8,544,128]{2,1,0:T(8,128)} %copy-done.1) | copy-start | bytes 6684676
  76.0 9.6 %collective-permute-start.4 = (f32[272,128]{1,0:T(8,128)S(1)}, f32[272,128]{1,0:T(8,128)S(1)}, u32[]{:S(2)}, u32[]{:S(2)}) collective-permute-start(f32[272,128]{1,0:T(8,128)S(1)} %get-tuple-element.41.left), channel_id=1, source_target_pairs={{1,0},{2,1},{3,2},{4,3},{5,4},{6,5},{7,6},{9,8},{10,9},{11,10},{12... | collective-permute-start | bytes 417800 | tf_op jit(solution)/shard_map/ppermute | solution.py:491
  78.0 7.5 %collective-permute-start.5 = (f32[272,128]{1,0:T(8,128)S(1)}, f32[272,128]{1,0:T(8,128)S(1)}, u32[]{:S(2)}, u32[]{:S(2)}) collective-permute-start(f32[272,128]{1,0:T(8,128)S(1)} %get-tuple-element.42.right), channel_id=1, source_target_pairs={{0,1},{1,2},{2,3},{3,4},{4,5},{5,6},{6,7},{8,9},{9,10},{10,11},{11... | collective-permute-start | bytes 417800 | tf_op jit(solution)/shard_map/ppermute | solution.py:492
  85.6 1.7 %copy-start.6 = (f32[9,544,128]{2,1,0:T(8,128)S(1)}, f32[9,544,128]{2,1,0:T(8,128)}, u32[]{:S(2)}) copy-start(f32[9,544,128]{2,1,0:T(8,128)} %copy-done.5) | copy-start | bytes 7520260
  87.3 1.7 %copy-start.8 = (f32[9,544,128]{2,1,0:T(8,128)S(1)}, f32[9,544,128]{2,1,0:T(8,128)}, u32[]{:S(2)}) copy-start(f32[9,544,128]{2,1,0:T(8,128)} %copy-done.7) | copy-start | bytes 7520260
  89.0 1.7 %copy-start.10 = (f32[9,544,128]{2,1,0:T(8,128)S(1)}, f32[9,544,128]{2,1,0:T(8,128)}, u32[]{:S(2)}) copy-start(f32[9,544,128]{2,1,0:T(8,128)} %copy-done.9) | copy-start | bytes 7520260

commit v2 on v1

v2 whole, which is shorter than its diff:
```python
import functools

import jax
import jax.numpy as jnp
import numpy as np
from jax import lax
from jax.experimental import pallas as pl
from jax.experimental.pallas import tpu as pltpu
from jax.sharding import PartitionSpec as P

OMEGA = 0.5
BS = 128
TOP = 16
BOTTOM = 24
F32 = jnp.float32
VMEM = pl.BlockSpec(memory_space=pltpu.VMEM)
SMEM = pl.BlockSpec(memory_space=pltpu.SMEM)
ANY = pl.BlockSpec(memory_space=pl.ANY)
HBM = pl.BlockSpec(memory_space=pltpu.HBM)


def lanes():
    return lax.broadcasted_iota(jnp.int32, (8, BS), 1)


def subs():
    return lax.broadcasted_iota(jnp.int32, (8, BS), 0)


def stage_kernel(a, b, l, head, tail, tiles, sems):
    rows = a.shape[0]
    copies = []
    for i, ref in enumerate((a, b, l)):
        copies.append(pltpu.make_async_copy(ref.at[0:8, :], tiles.at[i], sems.at[i]))
        copies.append(
            pltpu.make_async_copy(ref.at[rows - 8 : rows, :], tiles.at[3 + i], sems.at[3 + i])
        )
    for copy in copies:
        copy.start()
    for copy in copies:
        copy.wait()
    sub = lax.broadcasted_iota(jnp.int32, (8, a.shape[1]), 0)
    head[...] = jnp.where(
        sub < 3,
        tiles[0],
        jnp.where(sub < 6, pltpu.roll(tiles[1], 3, 0), pltpu.roll(tiles[2], 6, 0)),
    )
    tail[...] = jnp.where(
        sub < 3,
        pltpu.roll(tiles[3], 3, 0),
        jnp.where(sub < 6, pltpu.roll(tiles[4], 6, 0), tiles[5]),
    )


def rank_of(source, size):
    return source >> (size.bit_length() - 1) if size & (size - 1) == 0 else lax.div(source, size)


def rest_of(source, size):
    return source & (size - 1) if size & (size - 1) == 0 else lax.rem(source, size)


def source_of(table, groups, row, g):
    return table[row, g // (groups // 2), g % (groups // 2)]


def slot_of(owners, position):
    hit = jnp.int32(0)
    for earlier in range(position):
        hit = hit | (owners[earlier] == owners[position]).astype(jnp.int32)
    return hit


def send_kernel(dims, table, field, out, blocks, strip, in_sems, out_sems, strip_sem):
    ranks, groups, per_device, segments = dims
    me = lax.axis_index("wide")
    wanted = []

    def fetch(w, slot, local):
        return pltpu.make_async_copy(field.at[local], blocks.at[w, slot], in_sems.at[w, slot])

    def send(w, slot):
        return pltpu.make_async_copy(
            blocks.at[w, slot], out.at[w, pl.ds(slot * BS, BS), :], out_sems.at[w, slot]
        )

    for w in range(ranks):
        low, high, any_hit = jnp.int32(0), jnp.int32(0), jnp.int32(0)
        sources = [source_of(table, groups, w, g) for g in range(groups)]
        hits = [rank_of(source, per_device * segments) == me for source in sources]
        for source, hit in zip(sources, hits):
            high = jnp.where(hit, source, high)
            any_hit = jnp.where(hit, 1, any_hit)
        for source, hit in zip(reversed(sources), reversed(hits)):
            low = jnp.where(hit, source, low)
        low, high = rest_of(low, per_device), rest_of(high, per_device)
        wanted.append(any_hit)

        @pl.when(any_hit == 1)
        def _():
            fetch(w, 0, low).start()
            fetch(w, 1, high).start()

    for w in range(ranks):

        @pl.when(wanted[w] == 1)
        def _():
            for slot in range(2):
                fetch(w, slot, 0).wait()
                send(w, slot).start()

    sub = subs()
    for w in range(ranks):
        up, down = max(w - 1, 0), min(w + 1, ranks - 1)
        strip[w, 0:8, :] = jnp.where(
            sub < 4,
            pltpu.roll(blocks[up, 0, BS - 8 : BS, :], 4, 0),
            blocks[up, 1, BS - 8 : BS, :],
        )
        strip[w, 8:16, :] = jnp.where(
            sub < 4, blocks[down, 0, 0:8, :], pltpu.roll(blocks[down, 1, 0:8, :], 4, 0)
        )
    copy = pltpu.make_async_copy(strip, out.at[:, 2 * BS : 2 * BS + 16, :], strip_sem)
    copy.start()
    for w in range(ranks):

        @pl.when(wanted[w] == 1)
        def _():
            for slot in range(2):
                send(w, slot).wait()

    copy.wait()


def take_kernel(dims, table, recv, left, middle, right, tiles, sems, tile_sems):
    ranks, groups, per_device, segments = dims
    gy_count = groups // 2
    me = lax.axis_index("wide")
    up, down = jnp.maximum(me - 1, 0), jnp.minimum(me + 1, ranks - 1)

    def owners_of(row):
        return [
            rank_of(source_of(table, groups, row, g), per_device * segments) for g in range(groups)
        ]

    mine, above, below = owners_of(me), owners_of(up), owners_of(down)

    def column(gy):
        if gy == 0:
            return left
        if gy == gy_count - 1:
            return right
        return middle.at[gy - 1]

    copies = []
    for gx in range(2):
        for gy in range(gy_count):
            g = gx * gy_count + gy
            start = pl.multiple_of(slot_of(mine, g) * BS, BS)
            copies.append(
                pltpu.make_async_copy(
                    recv.at[mine[g], pl.ds(start, BS), :],
                    column(gy).at[8 + gx * BS : 8 + (gx + 1) * BS, :],
                    sems.at[g],
                )
            )
    for gy in range(gy_count):
        copies.append(
            pltpu.make_async_copy(
                recv.at[above[gy_count + gy], 2 * BS : 2 * BS + 8, :],
                tiles.at[gy],
                tile_sems.at[gy],
            )
        )
        copies.append(
            pltpu.make_async_copy(
                recv.at[below[gy], 2 * BS + 8 : 2 * BS + 16, :],
                tiles.at[gy_count + gy],
                tile_sems.at[gy_count + gy],
            )
        )
    for copy in copies:
        copy.start()
    for copy in copies:
        copy.wait()
    for gy in range(gy_count):
        tile = tiles[gy]
        tile = jnp.where(slot_of(above, gy_count + gy) == 0, pltpu.roll(tile, 4, 0), tile)
        column(gy)[0:8, :] = jnp.where(me > 0, tile, 0.0)
        tile = tiles[gy_count + gy]
        tile = jnp.where(slot_of(below, gy) == 1, pltpu.roll(tile, 4, 0), tile)
        column(gy)[8 + 2 * BS : 16 + 2 * BS, :] = jnp.where(me < ranks - 1, tile, 0.0)


def turn(x, by):
    return pltpu.roll(x, by % BS, 1)


def swap_stage(tiles, bit, lane):
    high = (lane & bit) != 0
    partner = lane ^ bit
    done = list(tiles)
    for low in range(len(tiles)):
        if not low & bit:
            first, second = tiles[low], tiles[low | bit]
            moved = jnp.take_along_axis(jnp.where(high, first, second), partner, axis=1)
            done[low] = jnp.where(high, moved, first)
            done[low | bit] = jnp.where(high, second, moved)
    return done


def interleave(tiles, lane):
    for bit in (1, 2):
        tiles = swap_stage(tiles, bit, lane)
    return tiles


def right_of(ts, lane):
    side = ts[-1]
    source = jnp.where(lane < BS - 4, lane + 4, jnp.where(lane == BS - 1, 0, lane - (BS - 5)))
    done = []
    for first in range(0, len(ts) - 1, 4):
        group = ts[first : first + 4]
        edge = jnp.where(lane == 0, ts[first + 4], group[0])
        done += group[1:] + [jnp.take_along_axis(edge, source, axis=1)]
    return done + [turn(jnp.where(lane == 0, ts[0], side), -1)]


def left_of(ts, lane):
    side = ts[-1]
    source = jnp.where(lane >= 4, lane - 4, jnp.where(lane == 0, BS - 1, lane + (BS - 5)))
    done = []
    for first in range(0, len(ts) - 1, 4):
        group = ts[first : first + 4]
        edge = jnp.where(lane == BS - 1, ts[first - 1], group[3])
        done += [jnp.take_along_axis(edge, source, axis=1)] + group[:3]
    return done + [turn(jnp.where(lane == BS - 1, ts[-2], side), 1)]


def spacing(dims, table, row, g):
    _, groups, per_device, segments = dims
    source = source_of(table, groups, row, g)
    level = table[rank_of(source, per_device * segments), 2, rest_of(source, per_device)]
    return jnp.where(level >= 1, F32(4.0), F32(1.0))


def halo_rows(dims, above, below, rows):
    me, ranks = lax.axis_index("wide"), dims[0]
    up, down = jnp.maximum(me - 1, 0), jnp.minimum(me + 1, ranks - 1)
    return (
        (TOP - 8, above, up, dims[1] // 2, (5, 2, 0)),
        (TOP + rows, below, down, 0, (0, 5, 2)),
    )


def pack_kernel(dims, table, a_in, b_in, l_in, above, below, to_left, to_right, raw, sems):
    rows, columns = a_in.shape
    gy_count = dims[1] // 2
    me = lax.axis_index("wide")
    copies = []
    for i, ref in enumerate((a_in, b_in, l_in)):
        for side, first in enumerate((0, columns - BS)):
            copies.append(
                pltpu.make_async_copy(
                    ref.at[:, first : first + BS], raw.at[side, i], sems.at[side, i]
                )
            )
    for copy in copies:
        copy.start()
    lane = lanes()

    def put_left(row, a, b, l):
        to_left[pl.ds(row, 8), :] = jnp.where(
            lane < 3, a, jnp.where(lane < 6, turn(b, 3), turn(l, 6))
        )

    def put_right(row, a, b, l):
        to_right[pl.ds(row, 8), :] = jnp.where(
            lane >= BS - 3, a, jnp.where(lane >= BS - 6, turn(b, -3), turn(l, -6))
        )

    for row, halo, base, at, turns in halo_rows(dims, above, below, rows):
        for put, first, gy in ((put_left, 0, 0), (put_right, columns - BS, gy_count - 1)):
            s = spacing(dims, table, base, at + gy)
            a, b, l = [pltpu.roll(halo[:, first : first + BS], by, 0) for by in turns]
            put(row, a * (0.5 * s), b * (s * s), l)
    for copy in copies:
        copy.wait()
    half = rows // 2
    for gx in range(2):
        s_left = spacing(dims, table, me, gx * gy_count)
        s_right = spacing(dims, table, me, gx * gy_count + gy_count - 1)

        def step(k, carry):
            row = pl.multiple_of(gx * half + 8 * k, 8)
            to = pl.multiple_of(row + TOP, 8)
            for side, put, s in ((0, put_left, s_left), (1, put_right, s_right)):
                a, b, l = [raw[side, i, pl.ds(row, 8), :] for i in range(3)]
                put(to, a * (0.5 * s), b * (s * s), l)
            return carry

        lax.fori_loop(0, half // 8, step, 0, unroll=4)


FX, FY, FYU, BEND, WEIGHT, LOAD = range(6)


def prep_kernel(
    dims, table, a_in, b_in, l_in, above, below, from_right, from_left, out, raw, a, k6, in_sems, out_sems
):
    ranks, groups, _, segments = dims
    gy_count = groups // 2
    planes = 2 * gy_count
    me, seg = lax.axis_index("wide"), lax.axis_index("narrow")
    rows = a_in.shape[0]
    chunks = in_sems.shape[1]
    size = rows // chunks
    lane, sub = lanes(), subs()
    strips = rows // 8 + 2
    near = lane < BS // 2
    cols = [slice(c * BS, (c + 1) * BS) for c in range(planes)]

    def read(i, chunk):
        ref = (a_in, b_in, l_in)[i]
        span = slice(chunk * size, (chunk + 1) * size)
        return pltpu.make_async_copy(ref.at[span, :], raw.at[i, span, :], in_sems.at[i, chunk])

    for chunk in range(chunks):
        for i in range(3):
            read(i, chunk).start()

    def side(k, carry):
        row = pl.multiple_of(TOP - 8 + 8 * k, 8)
        z = jnp.where(near, from_right[pl.ds(row, 8), :], from_left[pl.ds(row, 8), :])
        a[planes, pl.ds(row, 8), :] = z
        k6[BEND, planes, pl.ds(row, 8), :] = jnp.where(near, turn(z, -3), turn(z, 3))
        k6[LOAD, planes, pl.ds(row, 8), :] = jnp.where(near, turn(z, -6), turn(z, 6))
        return carry

    lax.fori_loop(0, strips, side, 0, unroll=6)

    def put(row, *arrays):
        for out_ref, tiles in zip((a, k6.at[BEND], k6.at[LOAD]), arrays):
            for c, tile in enumerate(interleave(tiles, lane)):
                out_ref[c, pl.ds(row, 8), :] = tile

    for row, halo, base, at, turns in halo_rows(dims, above, below, rows):
        s = [spacing(dims, table, base, at + gy) for gy in range(gy_count)]
        put(
            row,
            [pltpu.roll(halo[:, cols[c]], turns[0], 0) * (0.5 * s[c // 2]) for c in range(planes)],
            [pltpu.roll(halo[:, cols[c]], turns[1], 0) * (s[c // 2] * s[c // 2]) for c in range(planes)],
            [pltpu.roll(halo[:, cols[c]], turns[2], 0) for c in range(planes)],
        )
    for chunk in range(chunks):
        gx = 2 * chunk // chunks
        s = [spacing(dims, table, me, gx * gy_count + gy) for gy in range(gy_count)]
        for i in range(3):
            read(i, chunk).wait()

        def lay(k, carry):
            row = pl.multiple_of(chunk * size + k * 8, 8)
            put(
                pl.multiple_of(row + TOP, 8),
                [raw[0, pl.ds(row, 8), cols[c]] * (0.5 * s[c // 2]) for c in range(planes)],
                [raw[1, pl.ds(row, 8), cols[c]] * (s[c // 2] * s[c // 2]) for c in range(planes)],
                [raw[2, pl.ds(row, 8), cols[c]] for c in range(planes)],
            )
            return carry

        lax.fori_loop(0, size // 8, lay, 0, unroll=2)

    parts = out_sems.shape[1]
    part_size = strips // parts

    def write(i, part):
        span = slice(TOP - 8 + 8 * part * part_size, TOP - 8 + 8 * (part + 1) * part_size)
        return pltpu.make_async_copy(
            k6.at[i, :, span, :], out.at[i, :, span, :], out_sems.at[i, part]
        )

    for part in range(parts):
        for i in (BEND, LOAD):
            write(i, part).start()
    side_ok = ((lane < 2) & (seg < segments - 1)) | ((lane >= BS - 2) & (seg > 0))
    b = k6.at[BEND]

    def step(k, carry):
        row = pl.multiple_of(TOP - 8 + 8 * k, 8)
        at = [a[c, pl.ds(row, 8), :] for c in range(planes + 1)]
        bt = [b[c, pl.ds(row, 8), :] for c in range(planes + 1)]
        face = [x + y for x, y in zip(at, right_of(at, lane))]
        face_l = left_of(face, lane)
        bt_r, bt_l = right_of(bt, lane), left_of(bt, lane)
        here = row + sub
        row_ok = ((here >= TOP) | (me > 0)) & ((here < TOP + rows) | (me < ranks - 1))
        for c in range(planes + 1):
            below_face = at[c] + a[c, pl.ds(row + 1, 8), :]
            above_face = at[c] + a[c, pl.ds(row - 1, 8), :]
            near_b = b[c, pl.ds(row + 1, 8), :] + b[c, pl.ds(row - 1, 8), :] + bt_r[c] + bt_l[c]
            diag = 16.0 * bt[c] + face[c] + face_l[c] + below_face + above_face + near_b
            ok = row_ok & side_ok if c == planes else row_ok
            k6[FX, c, pl.ds(row, 8), :] = face[c]
            k6[FY, c, pl.ds(row, 8), :] = below_face
            k6[FYU, c, pl.ds(row, 8), :] = above_face
            k6[WEIGHT, c, pl.ds(row, 8), :] = jnp.where(ok, OMEGA / diag, 0.0)
        return carry

    for part in range(parts):
        lax.fori_loop(part * part_size, (part + 1) * part_size, step, 0, unroll=2)
        for i in (FX, FY, FYU, WEIGHT):
            write(i, part).start()
    for part in range(parts):
        for i in range(6):
            write(i, part).wait()


def split3(x):
    high = x.astype(jnp.bfloat16)
    rest = x - high.astype(F32)
    mid = rest.astype(jnp.bfloat16)
    low = (rest - mid.astype(F32)).astype(jnp.bfloat16)
    return jnp.concatenate([high, mid, low], axis=1)


def refine_rows(sources, put, strips):
    sub = subs()

    def step(k, carry):
        row = pl.multiple_of(8 * k, 8)
        part = lax.rem(k, 8)
        top, bottom = (sub == 0) & (part == 1), (sub == 7) & (part == 0)
        for c, src in enumerate(sources):
            x = src[pl.ds(row + 8, 8), :]
            up = jnp.where(top, x, src[pl.ds(row + 7, 8), :])
            down = jnp.where(bottom, x, src[pl.ds(row + 9, 8), :])
            near = 0.75 * x
            put(c, row, near + 0.25 * up, near + 0.25 * down)
        return carry

    lax.fori_loop(0, strips, step, 0, unroll=2)


def finish_kernel(
    group_weights, side_weights, left, middle, right, from_right, from_left, k_in,
    out, cols, edge, v, m, h, v1, k6, early_sems, late_sems,
):
    planes = cols.shape[0]
    gy_count = planes // 2
    coarse = left.shape[0]
    rows = out.shape[0]
    lane = lanes()
    chunks = early_sems.shape[1]
    strips = rows // 8 + 2
    size = strips // chunks

    def early(i, chunk):
        span = slice(TOP - 8 + 8 * chunk * size, TOP - 8 + 8 * (chunk + 1) * size)
        return pltpu.make_async_copy(
            k_in.at[i, :, span, :], k6.at[i, :, span, :], early_sems.at[i, chunk]
        )

    def late(i):
        span = slice(TOP - 8, TOP - 8 + 8 * strips)
        return pltpu.make_async_copy(
            k_in.at[i, :, span, :], k6.at[i, :, span, :], late_sems.at[i - WEIGHT]
        )

    for chunk in range(chunks):
        for i in (FX, FY, FYU, BEND):
            early(i, chunk).start()
    for i in (WEIGHT, LOAD):
        late(i).start()

    for gy in range(gy_count):
        parent = left[...] if gy == 0 else right[...] if gy == gy_count - 1 else middle[gy - 1]
        wide = jnp.dot(split3(parent), group_weights[...], preferred_element_type=F32)
        for half in range(2):
            cols[2 * gy + half, 8 : 8 + coarse, :] = wide[:, half * BS : (half + 1) * BS]
    wide_lane = lax.broadcasted_iota(jnp.int32, (coarse, BS), 1)
    beside = jnp.where(wide_lane < BS // 2, from_right[...], from_left[...])
    edge[8 : 8 + coarse, :] = jnp.dot(
        split3(beside), side_weights[...], preferred_element_type=F32
    )

    def mix(k, carry):
        row = pl.multiple_of(8 + 8 * k, 8)
        tiles = [cols[c, pl.ds(row, 8), :] for c in range(planes)]
        for c, tile in enumerate(swap_stage(tiles, 2, lane)):
            cols[c, pl.ds(row, 8), :] = tile
        return carry

    lax.fori_loop(0, coarse // 8, mix, 0, unroll=2)

    def put(c, row, even, odd):
        v[c, pl.ds(2 * row, 8, stride=2), :] = even
        v[c, pl.ds(2 * row + 1, 8, stride=2), :] = odd

    refine_rows([cols.at[c] for c in range(planes)] + [edge], put, coarse // 8)

    fx, fy, fyu, b, wt, l = [k6.at[i] for i in range(6)]

    def moments(u, waits):
        def step(k, carry):
            row = pl.multiple_of(TOP - 8 + 8 * k, 8)
            t = [u[c, pl.ds(row, 8), :] for c in range(planes + 1)]
            dx = [r - x for r, x in zip(right_of(t, lane), t)]
            q = [fx[c, pl.ds(row, 8), :] * dx[c] for c in range(planes + 1)]
            dxl, ql = left_of(dx, lane), left_of(q, lane)
            for c in range(planes + 1):
                dyd = u[c, pl.ds(row + 1, 8), :] - t[c]
                dyu = t[c] - u[c, pl.ds(row - 1, 8), :]
                lap = (dx[c] - dxl[c]) + (dyd - dyu)
                m[c, pl.ds(row, 8), :] = b[c, pl.ds(row, 8), :] * lap
                h[c, pl.ds(row, 8), :] = (q[c] - ql[c]) + (
                    fy[c, pl.ds(row, 8), :] * dyd - fyu[c, pl.ds(row, 8), :] * dyu
                )
            return carry

        for chunk in range(chunks if waits else 1):
            first, last = 0, strips
            if waits:
                first, last = chunk * size, (chunk + 1) * size
                for i in (FX, FY, FYU, BEND):
                    early(i, chunk).wait()
            lax.fori_loop(first, last, step, 0, unroll=2)

    def update(first, count, u, put, width, unroll):
        def step(k, carry):
            row = pl.multiple_of(first + 8 * k, 8)
            t = [m[c, pl.ds(row, 8), :] for c in range(planes + 1)]
            tr, tl = right_of(t, lane), left_of(t, lane)
            new = []
            for c in range(width):
                lap = (
                    tr[c] + tl[c] + m[c, pl.ds(row - 1, 8), :] + m[c, pl.ds(row + 1, 8), :]
                ) - 4.0 * t[c]
                rest = (l[c, pl.ds(row, 8), :] + h[c, pl.ds(row, 8), :]) - lap
                new.append(u[c, pl.ds(row, 8), :] + wt[c, pl.ds(row, 8), :] * rest)
            put(row, new)
            return carry

        lax.fori_loop(0, count, step, 0, unroll=unroll)

    def put_middle(row, new):
        for c, value in enumerate(new):
            v1[c, pl.ds(row, 8), :] = value

    def put_out(row, new):
        at = pl.multiple_of(row - TOP, 8)
        for c, value in enumerate(interleave(new, lane)):
            out[pl.ds(at, 8), c * BS : (c + 1) * BS] = value

    moments(v, True)
    for i in (WEIGHT, LOAD):
        late(i).wait()
    update(TOP - 8, strips, v, put_middle, planes + 1, 3)
    moments(v1, False)
    update(TOP, rows // 8, v1, put_out, planes, 4)


def quadrant_table(half_index):
    half_size = BS // 2
    row_ids, col_ids = np.arange(BS)[:, None], np.arange(BS)[None, :]
    base_cell = half_index * half_size
    near_cell = base_cell + row_ids // 2
    other_cell = near_cell + np.where(row_ids % 2 == 1, 1, -1)
    other_cell = np.clip(other_cell, base_cell, base_cell + half_size - 1)
    return 0.75 * (col_ids == near_cell) + 0.25 * (col_ids == other_cell)


def group_weights():
    low, high = quadrant_table(0).T, quadrant_table(1).T
    both = np.stack([low, high], axis=1).reshape(BS, 2, BS // 2, 2)
    both = both.transpose(0, 3, 2, 1).reshape(BS, 2 * BS)
    return jnp.asarray(np.concatenate([both] * 3), jnp.bfloat16)


def side_weights():
    low, high = quadrant_table(0).T, quadrant_table(1).T
    rim = np.where(np.arange(BS)[None, :] < BS // 2, low, high)
    return jnp.asarray(np.concatenate([rim] * 3), jnp.bfloat16)


def params(limit_mib):
    return pltpu.CompilerParams(vmem_limit_bytes=int(limit_mib * (1 << 20)))


def shape(*dims):
    return jax.ShapeDtypeStruct(dims, F32)


def local(old_field, old_level, new_source, stretch_coef, bend_coef, load_field):
    per_device = old_field.shape[0]
    groups_x, groups_y = new_source.shape
    groups = groups_x * groups_y
    ranks, segments = lax.axis_size("wide"), lax.axis_size("narrow")
    dims = (ranks, groups, per_device, segments)
    rows, columns = load_field.shape
    planes = columns // BS
    tall = rows + TOP + BOTTOM
    coarse = 2 * BS + 16
    up_links = [(i + 1, i) for i in range(ranks - 1)]
    down_links = [(i, i + 1) for i in range(ranks - 1)]
    left_links = [(i + 1, i) for i in range(segments - 1)]
    right_links = [(i, i + 1) for i in range(segments - 1)]

    facts = jnp.concatenate(
        [jnp.pad(new_source, ((0, 0), (0, per_device - groups_y))), old_level[None]]
    )
    table = lax.all_to_all(
        jnp.broadcast_to(facts[None], (ranks, *facts.shape)), "wide", 0, 0, tiled=True
    )

    head, tail = pl.pallas_call(
        stage_kernel,
        out_shape=[shape(8, columns), shape(8, columns)],
        in_specs=[HBM] * 3,
        out_specs=[VMEM] * 2,
        scratch_shapes=[pltpu.VMEM((6, 8, columns), F32), pltpu.SemaphoreType.DMA((6,))],
        compiler_params=params(62.3),
        name="stage_kernel",
    )(stretch_coef, bend_coef, load_field)
    above = lax.ppermute(tail, "wide", down_links)
    below = lax.ppermute(head, "wide", up_links)

    outgoing = pl.pallas_call(
        functools.partial(send_kernel, dims),
        out_shape=shape(ranks, coarse, BS),
        in_specs=[SMEM, HBM],
        out_specs=HBM,
        scratch_shapes=[
            pltpu.VMEM((ranks, 2, BS, BS), F32),
            pltpu.VMEM((ranks, 16, BS), F32),
            pltpu.SemaphoreType.DMA((ranks, 2)),
            pltpu.SemaphoreType.DMA((ranks, 2)),
            pltpu.SemaphoreType.DMA(()),
        ],
        compiler_params=params(62.3),
        name="send_build",
    )(table, old_field)
    incoming = lax.all_to_all(outgoing, "wide", 0, 0, tiled=True)

    to_left, to_right = pl.pallas_call(
        functools.partial(pack_kernel, dims),
        out_shape=[shape(tall, BS)] * 2,
        in_specs=[SMEM] + [HBM] * 3 + [VMEM] * 2,
        out_specs=[VMEM] * 2,
        scratch_shapes=[pltpu.VMEM((2, 3, rows, BS), F32), pltpu.SemaphoreType.DMA((2, 3))],
        compiler_params=params(62.3),
        name="pack",
    )(table, stretch_coef, bend_coef, load_field, above, below)
    from_right = lax.ppermute(to_left, "narrow", left_links)
    from_left = lax.ppermute(to_right, "narrow", right_links)
    coefs = pl.pallas_call(
        functools.partial(prep_kernel, dims),
        out_shape=shape(6, planes + 1, tall, BS),
        in_specs=[SMEM] + [HBM] * 3 + [VMEM] * 4,
        out_specs=HBM,
        scratch_shapes=[
            pltpu.VMEM((3, rows, columns), F32),
            pltpu.VMEM((planes + 1, tall, BS), F32),
            pltpu.VMEM((6, planes + 1, tall, BS), F32),
            pltpu.SemaphoreType.DMA((3, 4)),
            pltpu.SemaphoreType.DMA((6, 3)),
        ],
        compiler_params=params(62.3),
        name="prep_kernel",
    )(table, stretch_coef, bend_coef, load_field, above, below, from_right, from_left)

    left, middle, right = pl.pallas_call(
        functools.partial(take_kernel, dims),
        out_shape=[shape(coarse, BS), shape(groups_y - 2, coarse, BS), shape(coarse, BS)],
        in_specs=[SMEM, HBM],
        out_specs=[VMEM] * 3,
        scratch_shapes=[
            pltpu.VMEM((2 * groups_y, 8, BS), F32),
            pltpu.SemaphoreType.DMA((groups,)),
            pltpu.SemaphoreType.DMA((2 * groups_y,)),
        ],
        compiler_params=params(2),
        name="take",
    )(table, incoming)
    edge_right = lax.ppermute(left, "narrow", left_links)
    edge_left = lax.ppermute(right, "narrow", right_links)

    return pl.pallas_call(
        finish_kernel,
        out_shape=shape(rows, columns),
        in_specs=[VMEM] * 7 + [HBM],
        out_specs=VMEM,
        scratch_shapes=[
            pltpu.VMEM((planes, coarse + 16, BS), F32),
            pltpu.VMEM((coarse + 16, BS), F32),
        ]
        + [pltpu.VMEM((planes + 1, tall, BS), F32)] * 4
        + [
            pltpu.VMEM((6, planes + 1, tall, BS), F32),
            pltpu.SemaphoreType.DMA((4, 3)),
            pltpu.SemaphoreType.DMA((2,)),
        ],
        compiler_params=params(52),
        name="finish",
    )(group_weights(), side_weights(), left, middle, right, edge_right, edge_left, coefs)


def solution(mesh):
    return jax.shard_map(
        local,
        mesh=mesh,
        in_specs=(
            P(("wide", "narrow"), None, None),
            P(("wide", "narrow")),
            P("wide", "narrow"),
            P("wide", "narrow"),
            P("wide", "narrow"),
            P("wide", "narrow"),
        ),
        out_specs=P("wide", "narrow"),
        check_vma=False,
    )
```

time: 114 us -> 111 us (0.974)
  local copies, waits for them, and re-layouts: 22.5 us -> 2.65 us
  waiting for transfers between devices: 3.36 us -> 17.1 us
  blocking collectives: 9.28 us -> 11.5 us
    unnamed x30 -> x14, local copies, waits for them, and re-layouts: 20 us -> 2.64 us
    ppermute x1, waiting for transfers between devices: 0.01 us -> 17.1 us  [local(): above = lax.ppermute(tail, 'wide', down_links)]
    ppermute x1, waiting for transfers between devices: 2.46 us -> 0.01 us  [local(): from_right = lax.ppermute(to_left, 'narrow', left_links)]
    all_to_all x1, blocking collectives: 9.28 us -> 11.5 us  [local(): lax.all_to_all(jnp.broadcast_to(facts[None], (ranks, *facts.shape)), 'wid...]
    ppermute x1, starting transfers between devices: 4.69 us -> 6.53 us  [local(): from_right = lax.ppermute(to_left, 'narrow', left_links)]
    slice x3 -> x0, local copies, waits for them, and re-layouts: 1.68 us -> none  [the longest x2 1.6 us: local(): head = jnp.concatenate([stretch_coef[:3], bend_coef[:3], load_field[:2]])]
    pallas_call x1, Pallas kernels: 2.2 us -> 3.76 us  [local(): pl.pallas_call(functools.partial(send_kernel, dims), out_shape=shape(rank...]
    pallas_call x4, Pallas kernels: 44.5 us -> 43.4 us  [the longest x1 21.1 us: local(): pl.pallas_call(finish_kernel, out_shape=shape(rows, columns), in_specs=[V...]
  transfers between devices with their start and end apart: 7 -> 7, of which waited for: 2 -> 1; matrix products, arithmetic and copies ran while one was open for 2% -> 0% of each run, Pallas kernels for 20% -> 22%
where the time goes in v2:
time: 111 us; the launch traced here: 110 us
  Pallas kernels  49.5 us (45%)
  starting transfers between devices  28.8 us (26%)
  waiting for transfers between devices  17.1 us (15%)
  blocking collectives  11.5 us (10%)
  local copies, waits for them, and re-layouts  2.65 us (2%)
    pallas_call x1, Pallas kernels, local(): pl.pallas_call(finish_kernel, out_shape=shape(rows, columns), in_specs=[V...  21.1 us
    ppermute x1, waiting for transfers between devices, local(): above = lax.ppermute(tail, 'wide', down_links)  17.1 us
    pallas_call x1, Pallas kernels, local(): pl.pallas_call(functools.partial(prep_kernel, dims), out_shape=shape(6, p...  16 us
    all_to_all x1, blocking collectives, local(): lax.all_to_all(jnp.broadcast_to(facts[None], (ranks, *facts.shape)), 'wid...  11.5 us
    ppermute x1, starting transfers between devices, local(): from_right = lax.ppermute(to_left, 'narrow', left_links)  6.53 us
    all_to_all x1, starting transfers between devices, local(): incoming = lax.all_to_all(outgoing, 'wide', 0, 0, tiled=True)  5.99 us
    pallas_call x1, Pallas kernels, local(): pl.pallas_call(functools.partial(pack_kernel, dims), out_shape=[shape(tal...  4.82 us
    ppermute x1, starting transfers between devices, local(): below = lax.ppermute(head, 'wide', up_links)  4.29 us
  transfers between devices with their start and end apart: 7, of which 1 were waited for; matrix products, arithmetic and copies ran while one was open for 0% of the time, Pallas kernels for 22%

profile of v2, /device:TPU:7, one launch (start us, length us, event | category | flops | bytes accessed | tf_op | source)
XLA Modules:
  0.0 110.4 jit_solution(18198104420761304098)
XLA Ops:
  0.0 0.7 pad_add_fusion
  0.7 11.5 %all_to_all.10.table = s32[16,3,32]{2,1,0:T(4,128)} all-to-all(s32[16,3,32]{2,1,0:T(4,128)S(1)} %broadcast_in_dim.10), channel_id=1, replica_groups=mesh['wide'=16,'narrow'=8] {'wide'}, dimensions={0} | all-to-all | bytes 12288 | tf_op jit(solution)/shard_map/all_to_all | solution.py:611
  12.2 3.8 %send_build.1 = f32[16,272,128]{2,1,0:T(8,128)} custom-call(s32[16,3,32]{2,1,0:T(4,128)} %all_to_all.10.table, f32[32,128,128]{2,1,0:T(8,128)} %field.1), custom_call_target="tpu_custom_call" | custom-call | tf_op jit(solution)/shard_map/send_build/pallas_call | solution.py:627
  16.0 6.0 %all-to-all-start.1 = ((f32[16,272,128]{2,1,0:T(8,128)}), f32[16,272,128]{2,1,0:T(8,128)}, u32[]{:S(2)}, u32[]{:S(2)}) async-start(f32[16,272,128]{2,1,0:T(8,128)} %send_build.1), calls=%async_computation.1 | async-start | bytes 4456448 | tf_op jit(solution)/shard_map/all_to_all | solution.py:642
  22.0 1.5 %stage_kernel.1 = (f32[8,1024]{1,0:T(8,128)}, f32[8,1024]{1,0:T(8,128)}) custom-call(f32[512,1024]{1,0:T(8,128)} %a_in.3, f32[512,1024]{1,0:T(8,128)} %b_in.3, f32[512,1024]{1,0:T(8,128)} %l_in.3), custom_call_target="tpu_custom_call" | custom-call | tf_op jit(solution)/shard_map/stage_kernel/pallas_call | solution.py:615
  23.5 3.1 %collective-permute-start.2 = (f32[8,1024]{1,0:T(8,128)}, f32[8,1024]{1,0:T(8,128)S(1)}, u32[]{:S(2)}, u32[]{:S(2)}) collective-permute-start(f32[8,1024]{1,0:T(8,128)} %get-tuple-element.15), channel_id=1, source_target_pairs={{0,8},{8,16},{16,24},{24,32},{32,40},{40,48},{48,56},{56,64},{64,7... | collective-permute-start | bytes 98312 | tf_op jit(solution)/shard_map/ppermute | solution.py:624
  26.6 0.0 copy-start
  26.6 4.3 %collective-permute-start.3 = (f32[8,1024]{1,0:T(8,128)}, f32[8,1024]{1,0:T(8,128)S(1)}, u32[]{:S(2)}, u32[]{:S(2)}) collective-permute-start(f32[8,1024]{1,0:T(8,128)} %get-tuple-element.16), channel_id=1, source_target_pairs={{8,0},{16,8},{24,16},{32,24},{40,32},{48,40},{56,48},{64,56},{72,6... | collective-permute-start | bytes 98312 | tf_op jit(solution)/shard_map/ppermute | solution.py:625
  30.9 17.1 %collective-permute-done.2.above = f32[8,1024]{1,0:T(8,128)S(1)} collective-permute-done((f32[8,1024]{1,0:T(8,128)}, f32[8,1024]{1,0:T(8,128)S(1)}, u32[]{:S(2)}, u32[]{:S(2)}) %collective-permute-start.2) | collective-permute-done | bytes 32800 | tf_op jit(solution)/shard_map/ppermute | solution.py:624
  48.0 0.0 collective-permute-done.3.below
  48.0 0.6 copy-done.5
  48.6 0.6 copy-done.6
  49.2 4.8 %pack.1 = (f32[552,128]{1,0:T(8,128)}, f32[552,128]{1,0:T(8,128)}) custom-call(s32[16,3,32]{2,1,0:T(4,128)} %all_to_all.10.table, f32[512,1024]{1,0:T(8,128)} %a_in.3, f32[512,1024]{1,0:T(8,128)} %b_in.3, f32[512,1024]{1,0:T(8,128)} %l_in.3, f32[8,1024]{1,0:T(8,128)} %copy-done.5, f32[8,1024]{1,0:T(8,128)} %copy-done.6), custom_call_target="tpu_custom_call" | custom-call | tf_op jit(solution)/shard_map/pack/pallas_call | solution.py:644
  54.1 6.5 %collective-permute-start.4 = (f32[552,128]{1,0:T(8,128)}, f32[552,128]{1,0:T(8,128)S(1)}, u32[]{:S(2)}, u32[]{:S(2)}) collective-permute-start(f32[552,128]{1,0:T(8,128)} %get-tuple-element.17), channel_id=1, source_target_pairs={{1,0},{2,1},{3,2},{4,3},{5,4},{6,5},{7,6},{9,8},{10,9},{11,10},{12... | collective-permute-start | bytes 847880 | tf_op jit(solution)/shard_map/ppermute | solution.py:653
  60.6 3.2 %collective-permute-start.5 = (f32[552,128]{1,0:T(8,128)}, f32[552,128]{1,0:T(8,128)S(1)}, u32[]{:S(2)}, u32[]{:S(2)}) collective-permute-start(f32[552,128]{1,0:T(8,128)} %get-tuple-element.18), channel_id=1, source_target_pairs={{0,1},{1,2},{2,3},{3,4},{4,5},{5,6},{6,7},{8,9},{9,10},{10,11},{11... | collective-permute-start | bytes 847880 | tf_op jit(solution)/shard_map/ppermute | solution.py:654
  63.8 0.0 all-to-all-done.1.recv
  63.8 0.0 copy-done
  63.8 2.4 %take.1 = (f32[272,128]{1,0:T(8,128)S(1)}, f32[2,272,128]{2,1,0:T(8,128)S(1)}, f32[272,128]{1,0:T(8,128)S(1)}) custom-call(s32[16,3,32]{2,1,0:T(4,128)S(1)} %copy-done, f32[16,272,128]{2,1,0:T(8,128)} %all-to-all-done.1.recv), custom_call_target="tpu_custom_call" | custom-call | tf_op jit(solution)/shard_map/take/pallas_call | solution.py:671
  66.2 1.9 %collective-permute-start = (f32[272,128]{1,0:T(8,128)S(1)}, f32[272,128]{1,0:T(8,128)S(1)}, u32[]{:S(2)}, u32[]{:S(2)}) collective-permute-start(f32[272,128]{1,0:T(8,128)S(1)} %get-tuple-element.12.left), channel_id=1, source_target_pairs={{1,0},{2,1},{3,2},{4,3},{5,4},{6,5},{7,6},{9,8},{10,9},{11,10},{12... | collective-permute-start | bytes 417800 | tf_op jit(solution)/shard_map/ppermute | solution.py:684
  68.1 0.0 copy-start.1
  68.1 0.0 copy-start.2
  68.1 3.8 %collective-permute-start.1 = (f32[272,128]{1,0:T(8,128)S(1)}, f32[272,128]{1,0:T(8,128)S(1)}, u32[]{:S(2)}, u32[]{:S(2)}) collective-permute-start(f32[272,128]{1,0:T(8,128)S(1)} %get-tuple-element.14.right), channel_id=1, source_target_pairs={{0,1},{1,2},{2,3},{3,4},{4,5},{5,6},{6,7},{8,9},{9,10},{10,11},{11... | collective-permute-start | bytes 417800 | tf_op jit(solution)/shard_map/ppermute | solution.py:685
  71.9 0.0 collective-permute-done.4.from_right
  71.9 0.0 copy-start.3
  71.9 0.0 collective-permute-done.5.from_left
  71.9 0.7 copy-done.3
  72.6 0.7 copy-done.4
  73.3 16.0 %prep_kernel.1.k_in = f32[6,9,552,128]{3,2,1,0:T(8,128)} custom-call(s32[16,3,32]{2,1,0:T(4,128)} %all_to_all.10.table, f32[512,1024]{1,0:T(8,128)} %a_in.3, f32[512,1024]{1,0:T(8,128)} %b_in.3, f32[512,1024]{1,0:T(8,128)} %l_in.3, f32[8,1024]{1,0:T(8,128)} %copy-done.5, f32[8,1024]{1,0:T(8,128)} %copy-done.6, f32[552,128]{1,0:T(8,128)} %copy-done.3, ...), custom_call_target="tpu_custom_call" | custom-call | tf_op jit(solution)/shard_map/prep_kernel/pallas_call | solution.py:655
  89.3 0.0 collective-permute-done.from_right
  89.3 0.0 collective-permute-done.1.from_left
  89.3 0.0 copy-done.1
  89.4 21.1 %finish.1 = f32[512,1024]{1,0:T(8,128)} custom-call(bf16[384,256]{1,0:T(8,128)(2,1)S(1)} %copy-done.1, bf16[384,128]{1,0:T(8,128)(2,1)S(1)} %copy-done.2, f32[272,128]{1,0:T(8,128)S(1)} %get-tuple-element.12.left, f32[2,272,128]{2,1,0:T(8,128)S(1)} %get-tuple-element.13.middle, f32[272,128]{1,0:T(8,128)S(1)} %get-tuple-element.14.right, ...), custom_call_target="tpu_custom_call" | custom-call | tf_op jit(solution)/shard_map/finish/pallas_call | solution.py:687
  (5 shorter events, 0.0 us)
Async XLA Ops:
  16.0 47.8 %all-to-all-start.1 = ((f32[16,272,128]{2,1,0:T(8,128)}), f32[16,272,128]{2,1,0:T(8,128)}, u32[]{:S(2)}, u32[]{:S(2)}) async-start(f32[16,272,128]{2,1,0:T(8,128)} %send_build.1), calls=%async_computation.1 | async-start | bytes 4456448 | tf_op jit(solution)/shard_map/all_to_all | solution.py:642
  23.5 24.5 %collective-permute-start.2 = (f32[8,1024]{1,0:T(8,128)}, f32[8,1024]{1,0:T(8,128)S(1)}, u32[]{:S(2)}, u32[]{:S(2)}) collective-permute-start(f32[8,1024]{1,0:T(8,128)} %get-tuple-element.15), channel_id=1, source_target_pairs={{0,8},{8,16},{16,24},{24,32},{32,40},{40,48},{48,56},{56,64},{64,7... | collective-permute-start | bytes 98312 | tf_op jit(solution)/shard_map/ppermute | solution.py:624
  26.6 37.2 %copy-start = (s32[16,3,32]{2,1,0:T(4,128)S(1)}, s32[16,3,32]{2,1,0:T(4,128)}, u32[]{:S(2)}) copy-start(s32[16,3,32]{2,1,0:T(4,128)} %all_to_all.10.table) | copy-start | bytes 18436
  26.6 21.4 %collective-permute-start.3 = (f32[8,1024]{1,0:T(8,128)}, f32[8,1024]{1,0:T(8,128)S(1)}, u32[]{:S(2)}, u32[]{:S(2)}) collective-permute-start(f32[8,1024]{1,0:T(8,128)} %get-tuple-element.16), channel_id=1, source_target_pairs={{8,0},{16,8},{24,16},{32,24},{40,32},{48,40},{56,48},{64,56},{72,6... | collective-permute-start | bytes 98312 | tf_op jit(solution)/shard_map/ppermute | solution.py:625
  48.0 0.6 copy-start.5
  48.6 0.6 copy-start.6
  54.1 17.8 %collective-permute-start.4 = (f32[552,128]{1,0:T(8,128)}, f32[552,128]{1,0:T(8,128)S(1)}, u32[]{:S(2)}, u32[]{:S(2)}) collective-permute-start(f32[552,128]{1,0:T(8,128)} %get-tuple-element.17), channel_id=1, source_target_pairs={{1,0},{2,1},{3,2},{4,3},{5,4},{6,5},{7,6},{9,8},{10,9},{11,10},{12... | collective-permute-start | bytes 847880 | tf_op jit(solution)/shard_map/ppermute | solution.py:653
  60.6 11.3 %collective-permute-start.5 = (f32[552,128]{1,0:T(8,128)}, f32[552,128]{1,0:T(8,128)S(1)}, u32[]{:S(2)}, u32[]{:S(2)}) collective-permute-start(f32[552,128]{1,0:T(8,128)} %get-tuple-element.18), channel_id=1, source_target_pairs={{0,1},{1,2},{2,3},{3,4},{4,5},{5,6},{6,7},{8,9},{9,10},{10,11},{11... | collective-permute-start | bytes 847880 | tf_op jit(solution)/shard_map/ppermute | solution.py:654
  66.2 23.2 %collective-permute-start = (f32[272,128]{1,0:T(8,128)S(1)}, f32[272,128]{1,0:T(8,128)S(1)}, u32[]{:S(2)}, u32[]{:S(2)}) collective-permute-start(f32[272,128]{1,0:T(8,128)S(1)} %get-tuple-element.12.left), channel_id=1, source_target_pairs={{1,0},{2,1},{3,2},{4,3},{5,4},{6,5},{7,6},{9,8},{10,9},{11,10},{12... | collective-permute-start | bytes 417800 | tf_op jit(solution)/shard_map/ppermute | solution.py:684
  68.1 21.3 %copy-start.1 = (bf16[384,256]{1,0:T(8,128)(2,1)S(1)}, bf16[384,256]{1,0:T(8,128)(2,1)}, u32[]{:S(2)}) copy-start(bf16[384,256]{1,0:T(8,128)(2,1)} %constant.6.clone.group_weights) | copy-start | bytes 589828
  68.1 21.3 %copy-start.2 = (bf16[384,128]{1,0:T(8,128)(2,1)S(1)}, bf16[384,128]{1,0:T(8,128)(2,1)}, u32[]{:S(2)}) copy-start(bf16[384,128]{1,0:T(8,128)(2,1)} %constant.7.clone.side_weights) | copy-start | bytes 294916
  68.1 21.2 %collective-permute-start.1 = (f32[272,128]{1,0:T(8,128)S(1)}, f32[272,128]{1,0:T(8,128)S(1)}, u32[]{:S(2)}, u32[]{:S(2)}) collective-permute-start(f32[272,128]{1,0:T(8,128)S(1)} %get-tuple-element.14.right), channel_id=1, source_target_pairs={{0,1},{1,2},{2,3},{3,4},{4,5},{5,6},{6,7},{8,9},{9,10},{10,11},{11... | collective-permute-start | bytes 417800 | tf_op jit(solution)/shard_map/ppermute | solution.py:685
  71.9 0.7 copy-start.3
  72.6 0.7 copy-start.4

commit v3 on v2

--- a/solution.py
+++ b/solution.py
@@ -71,17 +71,14 @@
     return hit
 
 
-def send_kernel(dims, table, field, out, blocks, strip, in_sems, out_sems, strip_sem):
+def send_kernel(dims, table, field, out, strip, sems, strip_sem):
     ranks, groups, per_device, segments = dims
     me = lax.axis_index("wide")
-    wanted = []
-
-    def fetch(w, slot, local):
-        return pltpu.make_async_copy(field.at[local], blocks.at[w, slot], in_sems.at[w, slot])
-
-    def send(w, slot):
+    picked, wanted = [], []
+
+    def send(w, slot, local):
         return pltpu.make_async_copy(
-            blocks.at[w, slot], out.at[w, pl.ds(slot * BS, BS), :], out_sems.at[w, slot]
+            field.at[local], out.at[w, pl.ds(slot * BS, BS), :], sems.at[w, slot]
         )
 
     for w in range(ranks):
@@ -94,40 +91,33 @@
         for source, hit in zip(reversed(sources), reversed(hits)):
             low = jnp.where(hit, source, low)
         low, high = rest_of(low, per_device), rest_of(high, per_device)
+        picked.append((low, high))
         wanted.append(any_hit)
 
         @pl.when(any_hit == 1)
         def _():
-            fetch(w, 0, low).start()
-            fetch(w, 1, high).start()
-
+            send(w, 0, low).start()
+            send(w, 1, high).start()
+
+    sub = subs()
+    for w in range(ranks):
+        up, down = picked[max(w - 1, 0)], picked[min(w + 1, ranks - 1)]
+        strip[w, 0:8, :] = jnp.where(
+            sub < 4,
+            pltpu.roll(field[up[0], BS - 8 : BS, :], 4, 0),
+            field[up[1], BS - 8 : BS, :],
+        )
+        strip[w, 8:16, :] = jnp.where(
+            sub < 4, field[down[0], 0:8, :], pltpu.roll(field[down[1], 0:8, :], 4, 0)
+        )
+    copy = pltpu.make_async_copy(strip, out.at[:, 2 * BS : 2 * BS + 16, :], strip_sem)
+    copy.start()
     for w in range(ranks):
 
         @pl.when(wanted[w] == 1)
         def _():
             for slot in range(2):
-                fetch(w, slot, 0).wait()
-                send(w, slot).start()
-
-    sub = subs()
-    for w in range(ranks):
-        up, down = max(w - 1, 0), min(w + 1, ranks - 1)
-        strip[w, 0:8, :] = jnp.where(
-            sub < 4,
-            pltpu.roll(blocks[up, 0, BS - 8 : BS, :], 4, 0),
-            blocks[up, 1, BS - 8 : BS, :],
-        )
-        strip[w, 8:16, :] = jnp.where(
-            sub < 4, blocks[down, 0, 0:8, :], pltpu.roll(blocks[down, 1, 0:8, :], 4, 0)
-        )
-    copy = pltpu.make_async_copy(strip, out.at[:, 2 * BS : 2 * BS + 16, :], strip_sem)
-    copy.start()
-    for w in range(ranks):
-
-        @pl.when(wanted[w] == 1)
-        def _():
-            for slot in range(2):
-                send(w, slot).wait()
+                send(w, slot, 0).wait()
 
     copy.wait()
 
@@ -268,38 +258,43 @@
     for copy in copies:
         copy.start()
     lane = lanes()
-
-    def put_left(row, a, b, l):
-        to_left[pl.ds(row, 8), :] = jnp.where(
-            lane < 3, a, jnp.where(lane < 6, turn(b, 3), turn(l, 6))
-        )
-
-    def put_right(row, a, b, l):
-        to_right[pl.ds(row, 8), :] = jnp.where(
-            lane >= BS - 3, a, jnp.where(lane >= BS - 6, turn(b, -3), turn(l, -6))
-        )
-
-    for row, halo, base, at, turns in halo_rows(dims, above, below, rows):
-        for put, first, gy in ((put_left, 0, 0), (put_right, columns - BS, gy_count - 1)):
+    strips = rows // 8 + 2
+    per_tile = BS // 8
+    halos = halo_rows(dims, above, below, rows)
+
+    def strip_of(k, side):
+        gy = side * (gy_count - 1)
+        first = side * (columns - BS)
+        if 0 < k < strips - 1:
+            s = own[2 * (k - 1) // (strips - 2)][side]
+            a, b, l = [raw[side, i, 8 * (k - 1) : 8 * k, :] for i in range(3)]
+        else:
+            _, halo, base, at, turns = halos[0 if k == 0 else 1]
             s = spacing(dims, table, base, at + gy)
             a, b, l = [pltpu.roll(halo[:, first : first + BS], by, 0) for by in turns]
-            put(row, a * (0.5 * s), b * (s * s), l)
+        return a * (0.5 * s), b * (s * s), l
+
+    own = [
+        [spacing(dims, table, me, gx * gy_count + side * (gy_count - 1)) for side in range(2)]
+        for gx in range(2)
+    ]
     for copy in copies:
         copy.wait()
-    half = rows // 2
-    for gx in range(2):
-        s_left = spacing(dims, table, me, gx * gy_count)
-        s_right = spacing(dims, table, me, gx * gy_count + gy_count - 1)
-
-        def step(k, carry):
-            row = pl.multiple_of(gx * half + 8 * k, 8)
-            to = pl.multiple_of(row + TOP, 8)
-            for side, put, s in ((0, put_left, s_left), (1, put_right, s_right)):
-                a, b, l = [raw[side, i, pl.ds(row, 8), :] for i in range(3)]
-                put(to, a * (0.5 * s), b * (s * s), l)
-            return carry
-
-        lax.fori_loop(0, half // 8, step, 0, unroll=4)
+    for side, out in ((0, to_left), (1, to_right)):
+        sign = 1 - 2 * side
+        for tile in range(out.shape[0] // 8):
+            packed = jnp.zeros((8, BS), F32)
+            for slot in range(per_tile):
+                k = tile * per_tile + slot
+                if k >= strips:
+                    break
+                place = (lane - 8 * slot) & (BS - 1)
+                place = place if side == 0 else BS - 1 - place
+                a, b, l = strip_of(k, side)
+                packed = jnp.where(place < 3, turn(a, 8 * slot), packed)
+                packed = jnp.where((place >= 3) & (place < 6), turn(b, 8 * slot + 3 * sign), packed)
+                packed = jnp.where((place >= 6) & (place < 8), turn(l, 8 * slot + 6 * sign), packed)
+            out[8 * tile : 8 * tile + 8, :] = packed
 
 
 FX, FY, FYU, BEND, WEIGHT, LOAD = range(6)
@@ -329,15 +324,19 @@
         for i in range(3):
             read(i, chunk).start()
 
-    def side(k, carry):
-        row = pl.multiple_of(TOP - 8 + 8 * k, 8)
-        z = jnp.where(near, from_right[pl.ds(row, 8), :], from_left[pl.ds(row, 8), :])
-        a[planes, pl.ds(row, 8), :] = z
-        k6[BEND, planes, pl.ds(row, 8), :] = jnp.where(near, turn(z, -3), turn(z, 3))
-        k6[LOAD, planes, pl.ds(row, 8), :] = jnp.where(near, turn(z, -6), turn(z, 6))
-        return carry
-
-    lax.fori_loop(0, strips, side, 0, unroll=6)
+    per_tile = BS // 8
+    for k in range(strips):
+        tile, slot = k // per_tile, k % per_tile
+        at = slice(8 * tile, 8 * tile + 8)
+        z = jnp.where(((lane - 8 * slot) & (BS - 1)) < 8, from_right[at, :], from_left[at, :])
+        here = slice(TOP - 8 + 8 * k, TOP + 8 * k)
+        a[planes, here, :] = turn(z, -8 * slot)
+        k6[BEND, planes, here, :] = jnp.where(
+            near, turn(z, -8 * slot - 3), turn(z, -8 * slot + 3)
+        )
+        k6[LOAD, planes, here, :] = jnp.where(
+            near, turn(z, -8 * slot - 6), turn(z, -8 * slot + 6)
+        )
 
     def put(row, *arrays):
         for out_ref, tiles in zip((a, k6.at[BEND], k6.at[LOAD]), arrays):
@@ -368,7 +367,7 @@
             )
             return carry
 
-        lax.fori_loop(0, size // 8, lay, 0, unroll=2)
+        lax.fori_loop(0, size // 8, lay, 0, unroll=4)
 
     parts = out_sems.shape[1]
     part_size = strips // parts
@@ -407,7 +406,7 @@
         return carry
 
     for part in range(parts):
-        lax.fori_loop(part * part_size, (part + 1) * part_size, step, 0, unroll=2)
+        lax.fori_loop(part * part_size, (part + 1) * part_size, step, 0, unroll=11)
         for i in (FX, FY, FYU, WEIGHT):
             write(i, part).start()
     for part in range(parts):
@@ -523,7 +522,7 @@
                 first, last = chunk * size, (chunk + 1) * size
                 for i in (FX, FY, FYU, BEND):
                     early(i, chunk).wait()
-            lax.fori_loop(first, last, step, 0, unroll=2)
+            lax.fori_loop(first, last, step, 0, unroll=11)
 
     def update(first, count, u, put, width, unroll):
         def step(k, carry):
@@ -554,9 +553,9 @@
     moments(v, True)
     for i in (WEIGHT, LOAD):
         late(i).wait()
-    update(TOP - 8, strips, v, put_middle, planes + 1, 3)
+    update(TOP - 8, strips, v, put_middle, planes + 1, 11)
     moments(v1, False)
-    update(TOP, rows // 8, v1, put_out, planes, 4)
+    update(TOP, rows // 8, v1, put_out, planes, 8)
 
 
 def quadrant_table(half_index):
@@ -600,6 +599,7 @@
     planes = columns // BS
     tall = rows + TOP + BOTTOM
     coarse = 2 * BS + 16
+    packet = 8 * -(-(rows // 8 + 2) // (BS // 8))
     up_links = [(i + 1, i) for i in range(ranks - 1)]
     down_links = [(i, i + 1) for i in range(ranks - 1)]
     left_links = [(i + 1, i) for i in range(segments - 1)]
@@ -627,12 +627,10 @@
     outgoing = pl.pallas_call(
         functools.partial(send_kernel, dims),
         out_shape=shape(ranks, coarse, BS),
-        in_specs=[SMEM, HBM],
+        in_specs=[SMEM, VMEM],
         out_specs=HBM,
         scratch_shapes=[
-            pltpu.VMEM((ranks, 2, BS, BS), F32),
             pltpu.VMEM((ranks, 16, BS), F32),
-            pltpu.SemaphoreType.DMA((ranks, 2)),
             pltpu.SemaphoreType.DMA((ranks, 2)),
             pltpu.SemaphoreType.DMA(()),
         ],
@@ -643,7 +641,7 @@
 
     to_left, to_right = pl.pallas_call(
         functools.partial(pack_kernel, dims),
-        out_shape=[shape(tall, BS)] * 2,
+        out_shape=[shape(packet, BS)] * 2,
         in_specs=[SMEM] + [HBM] * 3 + [VMEM] * 2,
         out_specs=[VMEM] * 2,
         scratch_shapes=[pltpu.VMEM((2, 3, rows, BS), F32), pltpu.SemaphoreType.DMA((2, 3))],
@@ -696,7 +694,7 @@
         + [pltpu.VMEM((planes + 1, tall, BS), F32)] * 4
         + [
             pltpu.VMEM((6, planes + 1, tall, BS), F32),
-            pltpu.SemaphoreType.DMA((4, 3)),
+            pltpu.SemaphoreType.DMA((4, 2)),
             pltpu.SemaphoreType.DMA((2,)),
         ],
         compiler_params=params(52),

time: 111 us -> 110 us (level)
  the two profiles are of different devices: /device:TPU:7 before, /device:TPU:56 now
where the time goes in v3:
time: 110 us; the launch traced here: 109 us
  blocking collectives  45.1 us (41%)
  Pallas kernels  38.3 us (35%)
  starting transfers between devices  14.6 us (13%)
  waiting for transfers between devices  9.26 us (8%)
  local copies, waits for them, and re-layouts  1.26 us (1%)
    all_to_all x1, blocking collectives, local(): incoming = lax.all_to_all(outgoing, 'wide', 0, 0, tiled=True)  32.5 us
    pallas_call x1, Pallas kernels, local(): pl.pallas_call(functools.partial(prep_kernel, dims), out_shape=shape(6, p...  14.5 us
    pallas_call x1, Pallas kernels, local(): pl.pallas_call(finish_kernel, out_shape=shape(rows, columns), in_specs=[V...  13.5 us
    all_to_all x1, blocking collectives, local(): lax.all_to_all(jnp.broadcast_to(facts[None], (ranks, *facts.shape)), 'wid...  12.6 us
    ppermute x1, waiting for transfers between devices, local(): below = lax.ppermute(head, 'wide', up_links)  6.17 us
    ppermute x1, starting transfers between devices, local(): above = lax.ppermute(tail, 'wide', down_links)  3.8 us
    pallas_call x1, Pallas kernels, local(): pl.pallas_call(functools.partial(pack_kernel, dims), out_shape=[shape(pac...  3.69 us
    pallas_call x1, Pallas kernels, local(): pl.pallas_call(functools.partial(send_kernel, dims), out_shape=shape(rank...  2.92 us
  transfers between devices with their start and end apart: 6, of which 3 were waited for; matrix products, arithmetic and copies ran while one was open for 0% of the time, Pallas kernels for 18%

profile of v3, /device:TPU:56, one launch (start us, length us, event | category | flops | bytes accessed | tf_op | source)
XLA Modules:
  0.0 109.5 jit_solution(16705326902215298804)
XLA Ops:
  0.0 0.7 pad_add_fusion
  0.7 12.6 %all_to_all.10.table = s32[16,3,32]{2,1,0:T(4,128)} all-to-all(s32[16,3,32]{2,1,0:T(4,128)S(1)} %broadcast_in_dim.10), channel_id=1, replica_groups=mesh['wide'=16,'narrow'=8] {'wide'}, dimensions={0} | all-to-all | bytes 12288 | tf_op jit(solution)/shard_map/all_to_all | solution.py:611
  13.3 2.9 %send_build.1 = f32[16,272,128]{2,1,0:T(8,128)} custom-call(s32[16,3,32]{2,1,0:T(4,128)} %all_to_all.10.table, f32[32,128,128]{2,1,0:T(8,128)} %field.1), custom_call_target="tpu_custom_call" | custom-call | tf_op jit(solution)/shard_map/send_build/pallas_call | solution.py:627
  16.2 0.0 copy-start
  16.2 32.5 %all_to_all.11.recv = f32[16,272,128]{2,1,0:T(8,128)S(1)} all-to-all(f32[16,272,128]{2,1,0:T(8,128)} %send_build.1), channel_id=1, replica_groups=mesh['wide'=16,'narrow'=8] {'wide'}, dimensions={0} | all-to-all | bytes 4456448 | tf_op jit(solution)/shard_map/all_to_all | solution.py:640
  48.8 0.0 copy-done
  48.8 2.1 %take.1 = (f32[272,128]{1,0:T(8,128)S(1)}, f32[2,272,128]{2,1,0:T(8,128)S(1)}, f32[272,128]{1,0:T(8,128)S(1)}) custom-call(s32[16,3,32]{2,1,0:T(4,128)S(1)} %copy-done, f32[16,272,128]{2,1,0:T(8,128)S(1)} %all_to_all.11.recv), custom_call_target="tpu_custom_call" | custom-call | tf_op jit(solution)/shard_map/take/pallas_call | solution.py:669
  50.9 1.9 %collective-permute-start = (f32[272,128]{1,0:T(8,128)S(1)}, f32[272,128]{1,0:T(8,128)S(1)}, u32[]{:S(2)}, u32[]{:S(2)}) collective-permute-start(f32[272,128]{1,0:T(8,128)S(1)} %get-tuple-element.12.left), channel_id=1, source_target_pairs={{1,0},{2,1},{3,2},{4,3},{5,4},{6,5},{7,6},{9,8},{10,9},{11,10},{12... | collective-permute-start | bytes 417800 | tf_op jit(solution)/shard_map/ppermute | solution.py:682
  52.8 2.4 %collective-permute-start.1 = (f32[272,128]{1,0:T(8,128)S(1)}, f32[272,128]{1,0:T(8,128)S(1)}, u32[]{:S(2)}, u32[]{:S(2)}) collective-permute-start(f32[272,128]{1,0:T(8,128)S(1)} %get-tuple-element.14.right), channel_id=1, source_target_pairs={{0,1},{1,2},{2,3},{3,4},{4,5},{5,6},{6,7},{8,9},{9,10},{10,11},{11... | collective-permute-start | bytes 417800 | tf_op jit(solution)/shard_map/ppermute | solution.py:683
  55.2 1.5 %stage_kernel.1 = (f32[8,1024]{1,0:T(8,128)}, f32[8,1024]{1,0:T(8,128)}) custom-call(f32[512,1024]{1,0:T(8,128)} %a_in.3, f32[512,1024]{1,0:T(8,128)} %b_in.3, f32[512,1024]{1,0:T(8,128)} %l_in.3), custom_call_target="tpu_custom_call" | custom-call | tf_op jit(solution)/shard_map/stage_kernel/pallas_call | solution.py:615
  56.8 3.8 %collective-permute-start.2 = (f32[8,1024]{1,0:T(8,128)}, f32[8,1024]{1,0:T(8,128)S(1)}, u32[]{:S(2)}, u32[]{:S(2)}) collective-permute-start(f32[8,1024]{1,0:T(8,128)} %get-tuple-element.15), channel_id=1, source_target_pairs={{0,8},{8,16},{16,24},{24,32},{32,40},{40,48},{48,56},{56,64},{64,7... | collective-permute-start | bytes 98312 | tf_op jit(solution)/shard_map/ppermute | solution.py:624
  60.6 2.0 %collective-permute-start.3 = (f32[8,1024]{1,0:T(8,128)}, f32[8,1024]{1,0:T(8,128)S(1)}, u32[]{:S(2)}, u32[]{:S(2)}) collective-permute-start(f32[8,1024]{1,0:T(8,128)} %get-tuple-element.16), channel_id=1, source_target_pairs={{8,0},{16,8},{24,16},{32,24},{40,32},{48,40},{56,48},{64,56},{72,6... | collective-permute-start | bytes 98312 | tf_op jit(solution)/shard_map/ppermute | solution.py:625
  62.6 0.2 collective-permute-done.2.above
  62.8 6.2 %collective-permute-done.3.below = f32[8,1024]{1,0:T(8,128)S(1)} collective-permute-done((f32[8,1024]{1,0:T(8,128)}, f32[8,1024]{1,0:T(8,128)S(1)}, u32[]{:S(2)}, u32[]{:S(2)}) %collective-permute-start.3) | collective-permute-done | bytes 32800 | tf_op jit(solution)/shard_map/ppermute | solution.py:625
  69.0 0.0 copy-done.3
  69.0 0.6 copy-done.4
  69.6 3.7 %pack.1 = (f32[40,128]{1,0:T(8,128)}, f32[40,128]{1,0:T(8,128)}) custom-call(s32[16,3,32]{2,1,0:T(4,128)} %all_to_all.10.table, f32[512,1024]{1,0:T(8,128)} %a_in.3, f32[512,1024]{1,0:T(8,128)} %b_in.3, f32[512,1024]{1,0:T(8,128)} %l_in.3, f32[8,1024]{1,0:T(8,128)} %copy-done.3, f32[8,1024]{1,0:T(8,128)} %copy-done.4), custom_call_target="tpu_custom_call" | custom-call | tf_op jit(solution)/shard_map/pack/pallas_call | solution.py:642
  73.3 1.9 %collective-permute-start.4 = (f32[40,128]{1,0:T(8,128)}, f32[40,128]{1,0:T(8,128)S(1)}, u32[]{:S(2)}, u32[]{:S(2)}) collective-permute-start(f32[40,128]{1,0:T(8,128)} %get-tuple-element.17), channel_id=1, source_target_pairs={{1,0},{2,1},{3,2},{4,3},{5,4},{6,5},{7,6},{9,8},{10,9},{11,10},{12... | collective-permute-start | bytes 61448 | tf_op jit(solution)/shard_map/ppermute | solution.py:651
  75.3 0.0 copy-start.1
  75.3 0.0 copy-start.2
  75.3 2.5 %collective-permute-start.5 = (f32[40,128]{1,0:T(8,128)}, f32[40,128]{1,0:T(8,128)S(1)}, u32[]{:S(2)}, u32[]{:S(2)}) collective-permute-start(f32[40,128]{1,0:T(8,128)} %get-tuple-element.18), channel_id=1, source_target_pairs={{0,1},{1,2},{2,3},{3,4},{4,5},{5,6},{6,7},{8,9},{9,10},{10,11},{11... | collective-permute-start | bytes 61448 | tf_op jit(solution)/shard_map/ppermute | solution.py:652
  77.8 0.0 collective-permute-done.4.from_right
  77.8 0.0 copy-start.5
  77.8 2.9 %collective-permute-done.5.from_left = f32[40,128]{1,0:T(8,128)S(1)} collective-permute-done((f32[40,128]{1,0:T(8,128)}, f32[40,128]{1,0:T(8,128)S(1)}, u32[]{:S(2)}, u32[]{:S(2)}) %collective-permute-start.5) | collective-permute-done | bytes 20512 | tf_op jit(solution)/shard_map/ppermute | solution.py:652
  80.7 0.0 copy-done.5
  80.7 0.6 copy-done.6
  81.3 14.5 %prep_kernel.1.k_in = f32[6,9,552,128]{3,2,1,0:T(8,128)} custom-call(s32[16,3,32]{2,1,0:T(4,128)} %all_to_all.10.table, f32[512,1024]{1,0:T(8,128)} %a_in.3, f32[512,1024]{1,0:T(8,128)} %b_in.3, f32[512,1024]{1,0:T(8,128)} %l_in.3, f32[8,1024]{1,0:T(8,128)} %copy-done.3, f32[8,1024]{1,0:T(8,128)} %copy-done.4, f32[40,128]{1,0:T(8,128)} %copy-done.5, ...), custom_call_target="tpu_custom_call" | custom-call | tf_op jit(solution)/shard_map/prep_kernel/pallas_call | solution.py:653
  95.9 0.0 collective-permute-done.from_right
  95.9 0.0 collective-permute-done.1.from_left
  95.9 0.0 copy-done.1
  95.9 0.0 copy-done.2
  95.9 13.5 %finish.1 = f32[512,1024]{1,0:T(8,128)} custom-call(bf16[384,256]{1,0:T(8,128)(2,1)S(1)} %copy-done.1, bf16[384,128]{1,0:T(8,128)(2,1)S(1)} %copy-done.2, f32[272,128]{1,0:T(8,128)S(1)} %get-tuple-element.12.left, f32[2,272,128]{2,1,0:T(8,128)S(1)} %get-tuple-element.13.middle, f32[272,128]{1,0:T(8,128)S(1)} %get-tuple-element.14.right, ...), custom_call_target="tpu_custom_call" | custom-call | tf_op jit(solution)/shard_map/finish/pallas_call | solution.py:685
  (4 shorter events, 0.0 us)
Async XLA Ops:
  16.2 32.5 %copy-start = (s32[16,3,32]{2,1,0:T(4,128)S(1)}, s32[16,3,32]{2,1,0:T(4,128)}, u32[]{:S(2)}) copy-start(s32[16,3,32]{2,1,0:T(4,128)} %all_to_all.10.table) | copy-start | bytes 18436
  50.9 45.0 %collective-permute-start = (f32[272,128]{1,0:T(8,128)S(1)}, f32[272,128]{1,0:T(8,128)S(1)}, u32[]{:S(2)}, u32[]{:S(2)}) collective-permute-start(f32[272,128]{1,0:T(8,128)S(1)} %get-tuple-element.12.left), channel_id=1, source_target_pairs={{1,0},{2,1},{3,2},{4,3},{5,4},{6,5},{7,6},{9,8},{10,9},{11,10},{12... | collective-permute-start | bytes 417800 | tf_op jit(solution)/shard_map/ppermute | solution.py:682
  52.8 43.0 %collective-permute-start.1 = (f32[272,128]{1,0:T(8,128)S(1)}, f32[272,128]{1,0:T(8,128)S(1)}, u32[]{:S(2)}, u32[]{:S(2)}) collective-permute-start(f32[272,128]{1,0:T(8,128)S(1)} %get-tuple-element.14.right), channel_id=1, source_target_pairs={{0,1},{1,2},{2,3},{3,4},{4,5},{5,6},{6,7},{8,9},{9,10},{10,11},{11... | collective-permute-start | bytes 417800 | tf_op jit(solution)/shard_map/ppermute | solution.py:683
  56.8 6.1 %collective-permute-start.2 = (f32[8,1024]{1,0:T(8,128)}, f32[8,1024]{1,0:T(8,128)S(1)}, u32[]{:S(2)}, u32[]{:S(2)}) collective-permute-start(f32[8,1024]{1,0:T(8,128)} %get-tuple-element.15), channel_id=1, source_target_pairs={{0,8},{8,16},{16,24},{24,32},{32,40},{40,48},{48,56},{56,64},{64,7... | collective-permute-start | bytes 98312 | tf_op jit(solution)/shard_map/ppermute | solution.py:624
  60.6 8.4 %collective-permute-start.3 = (f32[8,1024]{1,0:T(8,128)}, f32[8,1024]{1,0:T(8,128)S(1)}, u32[]{:S(2)}, u32[]{:S(2)}) collective-permute-start(f32[8,1024]{1,0:T(8,128)} %get-tuple-element.16), channel_id=1, source_target_pairs={{8,0},{16,8},{24,16},{32,24},{40,32},{48,40},{56,48},{64,56},{72,6... | collective-permute-start | bytes 98312 | tf_op jit(solution)/shard_map/ppermute | solution.py:625
  62.8 6.2 %copy-start.3 = (f32[8,1024]{1,0:T(8,128)}, f32[8,1024]{1,0:T(8,128)S(1)}, u32[]{:S(2)}) copy-start(f32[8,1024]{1,0:T(8,128)S(1)} %collective-permute-done.2.above) | copy-start | bytes 98308
  69.0 0.6 copy-start.4
  73.3 4.5 %collective-permute-start.4 = (f32[40,128]{1,0:T(8,128)}, f32[40,128]{1,0:T(8,128)S(1)}, u32[]{:S(2)}, u32[]{:S(2)}) collective-permute-start(f32[40,128]{1,0:T(8,128)} %get-tuple-element.17), channel_id=1, source_target_pairs={{1,0},{2,1},{3,2},{4,3},{5,4},{6,5},{7,6},{9,8},{10,9},{11,10},{12... | collective-permute-start | bytes 61448 | tf_op jit(solution)/shard_map/ppermute | solution.py:651
  75.3 20.6 %copy-start.1 = (bf16[384,256]{1,0:T(8,128)(2,1)S(1)}, bf16[384,256]{1,0:T(8,128)(2,1)}, u32[]{:S(2)}) copy-start(bf16[384,256]{1,0:T(8,128)(2,1)} %constant.6.clone.group_weights) | copy-start | bytes 589828
  75.3 20.6 %copy-start.2 = (bf16[384,128]{1,0:T(8,128)(2,1)S(1)}, bf16[384,128]{1,0:T(8,128)(2,1)}, u32[]{:S(2)}) copy-start(bf16[384,128]{1,0:T(8,128)(2,1)} %constant.7.clone.side_weights) | copy-start | bytes 294916
  75.3 5.4 %collective-permute-start.5 = (f32[40,128]{1,0:T(8,128)}, f32[40,128]{1,0:T(8,128)S(1)}, u32[]{:S(2)}, u32[]{:S(2)}) collective-permute-start(f32[40,128]{1,0:T(8,128)} %get-tuple-element.18), channel_id=1, source_target_pairs={{0,1},{1,2},{2,3},{3,4},{4,5},{5,6},{6,7},{8,9},{9,10},{10,11},{11... | collective-permute-start | bytes 61448 | tf_op jit(solution)/shard_map/ppermute | solution.py:652
  77.8 2.9 %copy-start.5 = (f32[40,128]{1,0:T(8,128)}, f32[40,128]{1,0:T(8,128)S(1)}, u32[]{:S(2)}) copy-start(f32[40,128]{1,0:T(8,128)S(1)} %collective-permute-done.4.from_right) | copy-start | bytes 61444
  80.7 0.6 copy-start.6

commit v4 on v3

--- a/solution.py
+++ b/solution.py
@@ -297,11 +297,11 @@
             out[8 * tile : 8 * tile + 8, :] = packed
 
 
-FX, FY, FYU, BEND, WEIGHT, LOAD = range(6)
+FX, FY, BEND, WEIGHT, LOAD = range(5)
 
 
 def prep_kernel(
-    dims, table, a_in, b_in, l_in, above, below, from_right, from_left, out, raw, a, k6, in_sems, out_sems
+    dims, table, a_in, b_in, l_in, above, below, from_right, from_left, out, raw, a, kept, in_sems, out_sems
 ):
     ranks, groups, _, segments = dims
     gy_count = groups // 2
@@ -331,15 +331,15 @@
         z = jnp.where(((lane - 8 * slot) & (BS - 1)) < 8, from_right[at, :], from_left[at, :])
         here = slice(TOP - 8 + 8 * k, TOP + 8 * k)
         a[planes, here, :] = turn(z, -8 * slot)
-        k6[BEND, planes, here, :] = jnp.where(
+        kept[BEND, planes, here, :] = jnp.where(
             near, turn(z, -8 * slot - 3), turn(z, -8 * slot + 3)
         )
-        k6[LOAD, planes, here, :] = jnp.where(
+        kept[LOAD, planes, here, :] = jnp.where(
             near, turn(z, -8 * slot - 6), turn(z, -8 * slot + 6)
         )
 
     def put(row, *arrays):
-        for out_ref, tiles in zip((a, k6.at[BEND], k6.at[LOAD]), arrays):
+        for out_ref, tiles in zip((a, kept.at[BEND], kept.at[LOAD]), arrays):
             for c, tile in enumerate(interleave(tiles, lane)):
                 out_ref[c, pl.ds(row, 8), :] = tile
 
@@ -375,14 +375,14 @@
     def write(i, part):
         span = slice(TOP - 8 + 8 * part * part_size, TOP - 8 + 8 * (part + 1) * part_size)
         return pltpu.make_async_copy(
-            k6.at[i, :, span, :], out.at[i, :, span, :], out_sems.at[i, part]
+            kept.at[i, :, span, :], out.at[i, :, span, :], out_sems.at[i, part]
         )
 
     for part in range(parts):
         for i in (BEND, LOAD):
             write(i, part).start()
     side_ok = ((lane < 2) & (seg < segments - 1)) | ((lane >= BS - 2) & (seg > 0))
-    b = k6.at[BEND]
+    b = kept.at[BEND]
 
     def step(k, carry):
         row = pl.multiple_of(TOP - 8 + 8 * k, 8)
@@ -399,18 +399,17 @@
             near_b = b[c, pl.ds(row + 1, 8), :] + b[c, pl.ds(row - 1, 8), :] + bt_r[c] + bt_l[c]
             diag = 16.0 * bt[c] + face[c] + face_l[c] + below_face + above_face + near_b
             ok = row_ok & side_ok if c == planes else row_ok
-            k6[FX, c, pl.ds(row, 8), :] = face[c]
-            k6[FY, c, pl.ds(row, 8), :] = below_face
-            k6[FYU, c, pl.ds(row, 8), :] = above_face
-            k6[WEIGHT, c, pl.ds(row, 8), :] = jnp.where(ok, OMEGA / diag, 0.0)
+            kept[FX, c, pl.ds(row, 8), :] = face[c]
+            kept[FY, c, pl.ds(row, 8), :] = below_face
+            kept[WEIGHT, c, pl.ds(row, 8), :] = jnp.where(ok, OMEGA / diag, 0.0)
         return carry
 
     for part in range(parts):
         lax.fori_loop(part * part_size, (part + 1) * part_size, step, 0, unroll=11)
-        for i in (FX, FY, FYU, WEIGHT):
+        for i in (FX, FY, WEIGHT):
             write(i, part).start()
     for part in range(parts):
-        for i in range(6):
+        for i in range(5):
             write(i, part).wait()
 
 
@@ -442,7 +441,7 @@
 
 def finish_kernel(
     group_weights, side_weights, left, middle, right, from_right, from_left, k_in,
-    out, cols, edge, v, m, h, v1, k6, early_sems, late_sems,
+    out, cols, edge, v, m, h, v1, kept, early_sems, late_sems,
 ):
     planes = cols.shape[0]
     gy_count = planes // 2
@@ -456,17 +455,17 @@
     def early(i, chunk):
         span = slice(TOP - 8 + 8 * chunk * size, TOP - 8 + 8 * (chunk + 1) * size)
         return pltpu.make_async_copy(
-            k_in.at[i, :, span, :], k6.at[i, :, span, :], early_sems.at[i, chunk]
+            k_in.at[i, :, span, :], kept.at[i, :, span, :], early_sems.at[i, chunk]
         )
 
     def late(i):
         span = slice(TOP - 8, TOP - 8 + 8 * strips)
         return pltpu.make_async_copy(
-            k_in.at[i, :, span, :], k6.at[i, :, span, :], late_sems.at[i - WEIGHT]
+            k_in.at[i, :, span, :], kept.at[i, :, span, :], late_sems.at[i - WEIGHT]
         )
 
     for chunk in range(chunks):
-        for i in (FX, FY, FYU, BEND):
+        for i in (FX, FY, BEND):
             early(i, chunk).start()
     for i in (WEIGHT, LOAD):
         late(i).start()
@@ -497,7 +496,7 @@
 
     refine_rows([cols.at[c] for c in range(planes)] + [edge], put, coarse // 8)
 
-    fx, fy, fyu, b, wt, l = [k6.at[i] for i in range(6)]
+    fx, fy, b, wt, l = [kept.at[i] for i in range(5)]
 
     def moments(u, waits):
         def step(k, carry):
@@ -512,7 +511,7 @@
                 lap = (dx[c] - dxl[c]) + (dyd - dyu)
                 m[c, pl.ds(row, 8), :] = b[c, pl.ds(row, 8), :] * lap
                 h[c, pl.ds(row, 8), :] = (q[c] - ql[c]) + (
-                    fy[c, pl.ds(row, 8), :] * dyd - fyu[c, pl.ds(row, 8), :] * dyu
+                    fy[c, pl.ds(row, 8), :] * dyd - fy[c, pl.ds(row - 1, 8), :] * dyu
                 )
             return carry
 
@@ -520,7 +519,7 @@
             first, last = 0, strips
             if waits:
                 first, last = chunk * size, (chunk + 1) * size
-                for i in (FX, FY, FYU, BEND):
+                for i in (FX, FY, BEND):
                     early(i, chunk).wait()
             lax.fori_loop(first, last, step, 0, unroll=11)
 
@@ -652,15 +651,15 @@
     from_left = lax.ppermute(to_right, "narrow", right_links)
     coefs = pl.pallas_call(
         functools.partial(prep_kernel, dims),
-        out_shape=shape(6, planes + 1, tall, BS),
+        out_shape=shape(5, planes + 1, tall, BS),
         in_specs=[SMEM] + [HBM] * 3 + [VMEM] * 4,
         out_specs=HBM,
         scratch_shapes=[
             pltpu.VMEM((3, rows, columns), F32),
             pltpu.VMEM((planes + 1, tall, BS), F32),
-            pltpu.VMEM((6, planes + 1, tall, BS), F32),
+            pltpu.VMEM((5, planes + 1, tall, BS), F32),
             pltpu.SemaphoreType.DMA((3, 4)),
-            pltpu.SemaphoreType.DMA((6, 3)),
+            pltpu.SemaphoreType.DMA((5, 3)),
         ],
         compiler_params=params(62.3),
         name="prep_kernel",
@@ -693,8 +692,8 @@
         ]
         + [pltpu.VMEM((planes + 1, tall, BS), F32)] * 4
         + [
-            pltpu.VMEM((6, planes + 1, tall, BS), F32),
-            pltpu.SemaphoreType.DMA((4, 2)),
+            pltpu.VMEM((5, planes + 1, tall, BS), F32),
+            pltpu.SemaphoreType.DMA((3, 2)),
             pltpu.SemaphoreType.DMA((2,)),
         ],
         compiler_params=params(52),

time: 110 us -> 109 us (level)
  no operation moved by 1% of the time
where the time goes in v4:
time: 109 us
  blocking collectives  45.1 us (41%)
  Pallas kernels  37.4 us (34%)
  starting transfers between devices  14.6 us (13%)
  waiting for transfers between devices  9.26 us (8%)
  local copies, waits for them, and re-layouts  1.26 us (1%)
    all_to_all x1, blocking collectives, local(): incoming = lax.all_to_all(outgoing, 'wide', 0, 0, tiled=True)  32.4 us
    pallas_call x1, Pallas kernels, local(): pl.pallas_call(functools.partial(prep_kernel, dims), out_shape=shape(5, p...  14.3 us
    pallas_call x1, Pallas kernels, local(): pl.pallas_call(finish_kernel, out_shape=shape(rows, columns), in_specs=[V...  12.8 us
    all_to_all x1, blocking collectives, local(): lax.all_to_all(jnp.broadcast_to(facts[None], (ranks, *facts.shape)), 'wid...  12.8 us
    ppermute x1, waiting for transfers between devices, local(): below = lax.ppermute(head, 'wide', up_links)  6.17 us
    ppermute x1, starting transfers between devices, local(): above = lax.ppermute(tail, 'wide', down_links)  3.8 us
    pallas_call x1, Pallas kernels, local(): pl.pallas_call(functools.partial(pack_kernel, dims), out_shape=[shape(pac...  3.69 us
    pallas_call x1, Pallas kernels, local(): pl.pallas_call(functools.partial(send_kernel, dims), out_shape=shape(rank...  2.92 us
  transfers between devices with their start and end apart: 6, of which 3 were waited for; matrix products, arithmetic and copies ran while one was open for 0% of the time, Pallas kernels for 18%

profile of v4, /device:TPU:56, one launch (start us, length us, event | category | flops | bytes accessed | tf_op | source)
XLA Modules:
  0.0 108.5 jit_solution(2426109422532385734)
XLA Ops:
  0.0 0.7 pad_add_fusion
  0.7 12.8 %all_to_all.10.table = s32[16,3,32]{2,1,0:T(4,128)} all-to-all(s32[16,3,32]{2,1,0:T(4,128)S(1)} %broadcast_in_dim.10), channel_id=1, replica_groups=mesh['wide'=16,'narrow'=8] {'wide'}, dimensions={0} | all-to-all | bytes 12288 | tf_op jit(solution)/shard_map/all_to_all | solution.py:610
  13.5 2.9 %send_build.1 = f32[16,272,128]{2,1,0:T(8,128)} custom-call(s32[16,3,32]{2,1,0:T(4,128)} %all_to_all.10.table, f32[32,128,128]{2,1,0:T(8,128)} %field.1), custom_call_target="tpu_custom_call" | custom-call | tf_op jit(solution)/shard_map/send_build/pallas_call | solution.py:626
  16.4 0.0 copy-start
  16.4 32.4 %all_to_all.11.recv = f32[16,272,128]{2,1,0:T(8,128)S(1)} all-to-all(f32[16,272,128]{2,1,0:T(8,128)} %send_build.1), channel_id=1, replica_groups=mesh['wide'=16,'narrow'=8] {'wide'}, dimensions={0} | all-to-all | bytes 4456448 | tf_op jit(solution)/shard_map/all_to_all | solution.py:639
  48.8 0.0 copy-done
  48.8 2.1 %take.1 = (f32[272,128]{1,0:T(8,128)S(1)}, f32[2,272,128]{2,1,0:T(8,128)S(1)}, f32[272,128]{1,0:T(8,128)S(1)}) custom-call(s32[16,3,32]{2,1,0:T(4,128)S(1)} %copy-done, f32[16,272,128]{2,1,0:T(8,128)S(1)} %all_to_all.11.recv), custom_call_target="tpu_custom_call" | custom-call | tf_op jit(solution)/shard_map/take/pallas_call | solution.py:668
  50.9 1.9 %collective-permute-start = (f32[272,128]{1,0:T(8,128)S(1)}, f32[272,128]{1,0:T(8,128)S(1)}, u32[]{:S(2)}, u32[]{:S(2)}) collective-permute-start(f32[272,128]{1,0:T(8,128)S(1)} %get-tuple-element.12.left), channel_id=1, source_target_pairs={{1,0},{2,1},{3,2},{4,3},{5,4},{6,5},{7,6},{9,8},{10,9},{11,10},{12... | collective-permute-start | bytes 417800 | tf_op jit(solution)/shard_map/ppermute | solution.py:681
  52.8 2.4 %collective-permute-start.1 = (f32[272,128]{1,0:T(8,128)S(1)}, f32[272,128]{1,0:T(8,128)S(1)}, u32[]{:S(2)}, u32[]{:S(2)}) collective-permute-start(f32[272,128]{1,0:T(8,128)S(1)} %get-tuple-element.14.right), channel_id=1, source_target_pairs={{0,1},{1,2},{2,3},{3,4},{4,5},{5,6},{6,7},{8,9},{9,10},{10,11},{11... | collective-permute-start | bytes 417800 | tf_op jit(solution)/shard_map/ppermute | solution.py:682
  55.2 1.5 %stage_kernel.1 = (f32[8,1024]{1,0:T(8,128)}, f32[8,1024]{1,0:T(8,128)}) custom-call(f32[512,1024]{1,0:T(8,128)} %a_in.3, f32[512,1024]{1,0:T(8,128)} %b_in.3, f32[512,1024]{1,0:T(8,128)} %l_in.3), custom_call_target="tpu_custom_call" | custom-call | tf_op jit(solution)/shard_map/stage_kernel/pallas_call | solution.py:614
  56.8 3.8 %collective-permute-start.2 = (f32[8,1024]{1,0:T(8,128)}, f32[8,1024]{1,0:T(8,128)S(1)}, u32[]{:S(2)}, u32[]{:S(2)}) collective-permute-start(f32[8,1024]{1,0:T(8,128)} %get-tuple-element.15), channel_id=1, source_target_pairs={{0,8},{8,16},{16,24},{24,32},{32,40},{40,48},{48,56},{56,64},{64,7... | collective-permute-start | bytes 98312 | tf_op jit(solution)/shard_map/ppermute | solution.py:623
  60.6 2.0 %collective-permute-start.3 = (f32[8,1024]{1,0:T(8,128)}, f32[8,1024]{1,0:T(8,128)S(1)}, u32[]{:S(2)}, u32[]{:S(2)}) collective-permute-start(f32[8,1024]{1,0:T(8,128)} %get-tuple-element.16), channel_id=1, source_target_pairs={{8,0},{16,8},{24,16},{32,24},{40,32},{48,40},{56,48},{64,56},{72,6... | collective-permute-start | bytes 98312 | tf_op jit(solution)/shard_map/ppermute | solution.py:624
  62.6 0.2 collective-permute-done.2.above
  62.8 6.2 %collective-permute-done.3.below = f32[8,1024]{1,0:T(8,128)S(1)} collective-permute-done((f32[8,1024]{1,0:T(8,128)}, f32[8,1024]{1,0:T(8,128)S(1)}, u32[]{:S(2)}, u32[]{:S(2)}) %collective-permute-start.3) | collective-permute-done | bytes 32800 | tf_op jit(solution)/shard_map/ppermute | solution.py:624
  69.0 0.0 copy-done.3
  69.0 0.6 copy-done.4
  69.6 3.7 %pack.1 = (f32[40,128]{1,0:T(8,128)}, f32[40,128]{1,0:T(8,128)}) custom-call(s32[16,3,32]{2,1,0:T(4,128)} %all_to_all.10.table, f32[512,1024]{1,0:T(8,128)} %a_in.3, f32[512,1024]{1,0:T(8,128)} %b_in.3, f32[512,1024]{1,0:T(8,128)} %l_in.3, f32[8,1024]{1,0:T(8,128)} %copy-done.3, f32[8,1024]{1,0:T(8,128)} %copy-done.4), custom_call_target="tpu_custom_call" | custom-call | tf_op jit(solution)/shard_map/pack/pallas_call | solution.py:641
  73.3 1.9 %collective-permute-start.4 = (f32[40,128]{1,0:T(8,128)}, f32[40,128]{1,0:T(8,128)S(1)}, u32[]{:S(2)}, u32[]{:S(2)}) collective-permute-start(f32[40,128]{1,0:T(8,128)} %get-tuple-element.17), channel_id=1, source_target_pairs={{1,0},{2,1},{3,2},{4,3},{5,4},{6,5},{7,6},{9,8},{10,9},{11,10},{12... | collective-permute-start | bytes 61448 | tf_op jit(solution)/shard_map/ppermute | solution.py:650
  75.3 0.0 copy-start.1
  75.3 0.0 copy-start.2
  75.3 2.5 %collective-permute-start.5 = (f32[40,128]{1,0:T(8,128)}, f32[40,128]{1,0:T(8,128)S(1)}, u32[]{:S(2)}, u32[]{:S(2)}) collective-permute-start(f32[40,128]{1,0:T(8,128)} %get-tuple-element.18), channel_id=1, source_target_pairs={{0,1},{1,2},{2,3},{3,4},{4,5},{5,6},{6,7},{8,9},{9,10},{10,11},{11... | collective-permute-start | bytes 61448 | tf_op jit(solution)/shard_map/ppermute | solution.py:651
  77.8 0.0 collective-permute-done.4.from_right
  77.8 0.0 copy-start.5
  77.8 2.9 %collective-permute-done.5.from_left = f32[40,128]{1,0:T(8,128)S(1)} collective-permute-done((f32[40,128]{1,0:T(8,128)}, f32[40,128]{1,0:T(8,128)S(1)}, u32[]{:S(2)}, u32[]{:S(2)}) %collective-permute-start.5) | collective-permute-done | bytes 20512 | tf_op jit(solution)/shard_map/ppermute | solution.py:651
  80.7 0.0 copy-done.5
  80.7 0.6 copy-done.6
  81.3 14.3 %prep_kernel.1.k_in = f32[5,9,552,128]{3,2,1,0:T(8,128)} custom-call(s32[16,3,32]{2,1,0:T(4,128)} %all_to_all.10.table, f32[512,1024]{1,0:T(8,128)} %a_in.3, f32[512,1024]{1,0:T(8,128)} %b_in.3, f32[512,1024]{1,0:T(8,128)} %l_in.3, f32[8,1024]{1,0:T(8,128)} %copy-done.3, f32[8,1024]{1,0:T(8,128)} %copy-done.4, f32[40,128]{1,0:T(8,128)} %copy-done.5, ...), custom_call_target="tpu_custom_call" | custom-call | tf_op jit(solution)/shard_map/prep_kernel/pallas_call | solution.py:652
  95.6 0.0 collective-permute-done.from_right
  95.6 0.0 collective-permute-done.1.from_left
  95.7 0.0 copy-done.1
  95.7 0.0 copy-done.2
  95.7 12.8 %finish.1 = f32[512,1024]{1,0:T(8,128)} custom-call(bf16[384,256]{1,0:T(8,128)(2,1)S(1)} %copy-done.1, bf16[384,128]{1,0:T(8,128)(2,1)S(1)} %copy-done.2, f32[272,128]{1,0:T(8,128)S(1)} %get-tuple-element.12.left, f32[2,272,128]{2,1,0:T(8,128)S(1)} %get-tuple-element.13.middle, f32[272,128]{1,0:T(8,128)S(1)} %get-tuple-element.14.right, ...), custom_call_target="tpu_custom_call" | custom-call | tf_op jit(solution)/shard_map/finish/pallas_call | solution.py:684
  (4 shorter events, 0.0 us)
Async XLA Ops:
  16.4 32.4 %copy-start = (s32[16,3,32]{2,1,0:T(4,128)S(1)}, s32[16,3,32]{2,1,0:T(4,128)}, u32[]{:S(2)}) copy-start(s32[16,3,32]{2,1,0:T(4,128)} %all_to_all.10.table) | copy-start | bytes 18436
  50.9 44.7 %collective-permute-start = (f32[272,128]{1,0:T(8,128)S(1)}, f32[272,128]{1,0:T(8,128)S(1)}, u32[]{:S(2)}, u32[]{:S(2)}) collective-permute-start(f32[272,128]{1,0:T(8,128)S(1)} %get-tuple-element.12.left), channel_id=1, source_target_pairs={{1,0},{2,1},{3,2},{4,3},{5,4},{6,5},{7,6},{9,8},{10,9},{11,10},{12... | collective-permute-start | bytes 417800 | tf_op jit(solution)/shard_map/ppermute | solution.py:681
  52.8 42.8 %collective-permute-start.1 = (f32[272,128]{1,0:T(8,128)S(1)}, f32[272,128]{1,0:T(8,128)S(1)}, u32[]{:S(2)}, u32[]{:S(2)}) collective-permute-start(f32[272,128]{1,0:T(8,128)S(1)} %get-tuple-element.14.right), channel_id=1, source_target_pairs={{0,1},{1,2},{2,3},{3,4},{4,5},{5,6},{6,7},{8,9},{9,10},{10,11},{11... | collective-permute-start | bytes 417800 | tf_op jit(solution)/shard_map/ppermute | solution.py:682
  56.8 6.1 %collective-permute-start.2 = (f32[8,1024]{1,0:T(8,128)}, f32[8,1024]{1,0:T(8,128)S(1)}, u32[]{:S(2)}, u32[]{:S(2)}) collective-permute-start(f32[8,1024]{1,0:T(8,128)} %get-tuple-element.15), channel_id=1, source_target_pairs={{0,8},{8,16},{16,24},{24,32},{32,40},{40,48},{48,56},{56,64},{64,7... | collective-permute-start | bytes 98312 | tf_op jit(solution)/shard_map/ppermute | solution.py:623
  60.6 8.4 %collective-permute-start.3 = (f32[8,1024]{1,0:T(8,128)}, f32[8,1024]{1,0:T(8,128)S(1)}, u32[]{:S(2)}, u32[]{:S(2)}) collective-permute-start(f32[8,1024]{1,0:T(8,128)} %get-tuple-element.16), channel_id=1, source_target_pairs={{8,0},{16,8},{24,16},{32,24},{40,32},{48,40},{56,48},{64,56},{72,6... | collective-permute-start | bytes 98312 | tf_op jit(solution)/shard_map/ppermute | solution.py:624
  62.8 6.2 %copy-start.3 = (f32[8,1024]{1,0:T(8,128)}, f32[8,1024]{1,0:T(8,128)S(1)}, u32[]{:S(2)}) copy-start(f32[8,1024]{1,0:T(8,128)S(1)} %collective-permute-done.2.above) | copy-start | bytes 98308
  69.0 0.6 copy-start.4
  73.3 4.5 %collective-permute-start.4 = (f32[40,128]{1,0:T(8,128)}, f32[40,128]{1,0:T(8,128)S(1)}, u32[]{:S(2)}, u32[]{:S(2)}) collective-permute-start(f32[40,128]{1,0:T(8,128)} %get-tuple-element.17), channel_id=1, source_target_pairs={{1,0},{2,1},{3,2},{4,3},{5,4},{6,5},{7,6},{9,8},{10,9},{11,10},{12... | collective-permute-start | bytes 61448 | tf_op jit(solution)/shard_map/ppermute | solution.py:650
  75.3 20.4 %copy-start.1 = (bf16[384,256]{1,0:T(8,128)(2,1)S(1)}, bf16[384,256]{1,0:T(8,128)(2,1)}, u32[]{:S(2)}) copy-start(bf16[384,256]{1,0:T(8,128)(2,1)} %constant.6.clone.group_weights) | copy-start | bytes 589828
  75.3 20.4 %copy-start.2 = (bf16[384,128]{1,0:T(8,128)(2,1)S(1)}, bf16[384,128]{1,0:T(8,128)(2,1)}, u32[]{:S(2)}) copy-start(bf16[384,128]{1,0:T(8,128)(2,1)} %constant.7.clone.side_weights) | copy-start | bytes 294916
  75.3 5.4 %collective-permute-start.5 = (f32[40,128]{1,0:T(8,128)}, f32[40,128]{1,0:T(8,128)S(1)}, u32[]{:S(2)}, u32[]{:S(2)}) collective-permute-start(f32[40,128]{1,0:T(8,128)} %get-tuple-element.18), channel_id=1, source_target_pairs={{0,1},{1,2},{2,3},{3,4},{4,5},{5,6},{6,7},{8,9},{9,10},{10,11},{11... | collective-permute-start | bytes 61448 | tf_op jit(solution)/shard_map/ppermute | solution.py:651
  77.8 2.9 %copy-start.5 = (f32[40,128]{1,0:T(8,128)}, f32[40,128]{1,0:T(8,128)S(1)}, u32[]{:S(2)}) copy-start(f32[40,128]{1,0:T(8,128)S(1)} %collective-permute-done.4.from_right) | copy-start | bytes 61444
  80.7 0.6 copy-start.6

commit v5 on v4

--- a/solution.py
+++ b/solution.py
@@ -617,7 +617,7 @@
         in_specs=[HBM] * 3,
         out_specs=[VMEM] * 2,
         scratch_shapes=[pltpu.VMEM((6, 8, columns), F32), pltpu.SemaphoreType.DMA((6,))],
-        compiler_params=params(62.3),
+        compiler_params=params(52.3),
         name="stage_kernel",
     )(stretch_coef, bend_coef, load_field)
     above = lax.ppermute(tail, "wide", down_links)
@@ -633,7 +633,7 @@
             pltpu.SemaphoreType.DMA((ranks, 2)),
             pltpu.SemaphoreType.DMA(()),
         ],
-        compiler_params=params(62.3),
+        compiler_params=params(52.3),
         name="send_build",
     )(table, old_field)
     incoming = lax.all_to_all(outgoing, "wide", 0, 0, tiled=True)
@@ -644,7 +644,7 @@
         in_specs=[SMEM] + [HBM] * 3 + [VMEM] * 2,
         out_specs=[VMEM] * 2,
         scratch_shapes=[pltpu.VMEM((2, 3, rows, BS), F32), pltpu.SemaphoreType.DMA((2, 3))],
-        compiler_params=params(62.3),
+        compiler_params=params(52.3),
         name="pack",
     )(table, stretch_coef, bend_coef, load_field, above, below)
     from_right = lax.ppermute(to_left, "narrow", left_links)
@@ -661,7 +661,7 @@
             pltpu.SemaphoreType.DMA((3, 4)),
             pltpu.SemaphoreType.DMA((5, 3)),
         ],
-        compiler_params=params(62.3),
+        compiler_params=params(52.3),
         name="prep_kernel",
     )(table, stretch_coef, bend_coef, load_field, above, below, from_right, from_left)
 

time: 109 us -> 106 us (0.972)
  Pallas kernels: 37.4 us -> 35.9 us
  local copies, waits for them, and re-layouts: 1.26 us -> 0.02 us
    unnamed x14 -> x4, local copies, waits for them, and re-layouts: 1.25 us -> 0.01 us
  transfers between devices with their start and end apart: 6 -> 6, of which waited for: 3 -> 2; matrix products, arithmetic and copies ran while one was open for 0% -> 0% of each run, Pallas kernels for 18% -> 17%
where the time goes in v5:
time: 106 us; the launch traced here: 105 us
  blocking collectives  45 us (42%)
  Pallas kernels  35.9 us (34%)
  starting transfers between devices  14.6 us (14%)
  waiting for transfers between devices  8.85 us (8%)
    all_to_all x1, blocking collectives, local(): incoming = lax.all_to_all(outgoing, 'wide', 0, 0, tiled=True)  32.3 us
    pallas_call x1, Pallas kernels, local(): pl.pallas_call(functools.partial(prep_kernel, dims), out_shape=shape(5, p...  14.1 us
    pallas_call x1, Pallas kernels, local(): pl.pallas_call(finish_kernel, out_shape=shape(rows, columns), in_specs=[V...  12.8 us
    all_to_all x1, blocking collectives, local(): lax.all_to_all(jnp.broadcast_to(facts[None], (ranks, *facts.shape)), 'wid...  12.7 us
    ppermute x1, waiting for transfers between devices, local(): below = lax.ppermute(head, 'wide', up_links)  6.16 us
    ppermute x1, starting transfers between devices, local(): above = lax.ppermute(tail, 'wide', down_links)  3.81 us
    pallas_call x1, Pallas kernels, local(): pl.pallas_call(functools.partial(pack_kernel, dims), out_shape=[shape(pac...  2.96 us
    pallas_call x1, Pallas kernels, local(): pl.pallas_call(functools.partial(send_kernel, dims), out_shape=shape(rank...  2.94 us
  transfers between devices with their start and end apart: 6, of which 2 were waited for; matrix products, arithmetic and copies ran while one was open for 0% of the time, Pallas kernels for 17%

profile of v5, /device:TPU:56, one launch (start us, length us, event | category | flops | bytes accessed | tf_op | source)
XLA Modules:
  0.0 105.2 jit_solution(9924039694479259322)
XLA Ops:
  0.0 0.7 pad_add_fusion
  0.7 12.7 %all_to_all.10.table = s32[16,3,32]{2,1,0:T(4,128)S(1)} all-to-all(s32[16,3,32]{2,1,0:T(4,128)S(1)} %broadcast_in_dim.10), channel_id=1, replica_groups=mesh['wide'=16,'narrow'=8] {'wide'}, dimensions={0} | all-to-all | bytes 12288 | tf_op jit(solution)/shard_map/all_to_all | solution.py:610
  13.4 2.9 %send_build.1 = f32[16,272,128]{2,1,0:T(8,128)} custom-call(s32[16,3,32]{2,1,0:T(4,128)S(1)} %all_to_all.10.table, f32[32,128,128]{2,1,0:T(8,128)} %field.1), custom_call_target="tpu_custom_call" | custom-call | tf_op jit(solution)/shard_map/send_build/pallas_call | solution.py:626
  16.3 32.3 %all_to_all.11.recv = f32[16,272,128]{2,1,0:T(8,128)S(1)} all-to-all(f32[16,272,128]{2,1,0:T(8,128)} %send_build.1), channel_id=1, replica_groups=mesh['wide'=16,'narrow'=8] {'wide'}, dimensions={0} | all-to-all | bytes 4456448 | tf_op jit(solution)/shard_map/all_to_all | solution.py:639
  48.7 2.1 %take.1 = (f32[272,128]{1,0:T(8,128)S(1)}, f32[2,272,128]{2,1,0:T(8,128)S(1)}, f32[272,128]{1,0:T(8,128)S(1)}) custom-call(s32[16,3,32]{2,1,0:T(4,128)S(1)} %all_to_all.10.table, f32[16,272,128]{2,1,0:T(8,128)S(1)} %all_to_all.11.recv), custom_call_target="tpu_custom_call" | custom-call | tf_op jit(solution)/shard_map/take/pallas_call | solution.py:668
  50.8 1.9 %collective-permute-start = (f32[272,128]{1,0:T(8,128)S(1)}, f32[272,128]{1,0:T(8,128)S(1)}, u32[]{:S(2)}, u32[]{:S(2)}) collective-permute-start(f32[272,128]{1,0:T(8,128)S(1)} %get-tuple-element.12.left), channel_id=1, source_target_pairs={{1,0},{2,1},{3,2},{4,3},{5,4},{6,5},{7,6},{9,8},{10,9},{11,10},{12... | collective-permute-start | bytes 417800 | tf_op jit(solution)/shard_map/ppermute | solution.py:681
  52.7 2.4 %collective-permute-start.1 = (f32[272,128]{1,0:T(8,128)S(1)}, f32[272,128]{1,0:T(8,128)S(1)}, u32[]{:S(2)}, u32[]{:S(2)}) collective-permute-start(f32[272,128]{1,0:T(8,128)S(1)} %get-tuple-element.14.right), channel_id=1, source_target_pairs={{0,1},{1,2},{2,3},{3,4},{4,5},{5,6},{6,7},{8,9},{9,10},{10,11},{11... | collective-permute-start | bytes 417800 | tf_op jit(solution)/shard_map/ppermute | solution.py:682
  55.1 0.9 stage_kernel.1
  56.0 3.8 %collective-permute-start.2 = (f32[8,1024]{1,0:T(8,128)S(1)}, f32[8,1024]{1,0:T(8,128)S(1)}, u32[]{:S(2)}, u32[]{:S(2)}) collective-permute-start(f32[8,1024]{1,0:T(8,128)S(1)} %get-tuple-element.15), channel_id=1, source_target_pairs={{0,8},{8,16},{16,24},{24,32},{32,40},{40,48},{48,56},{56,64},{64,7... | collective-permute-start | bytes 98312 | tf_op jit(solution)/shard_map/ppermute | solution.py:623
  59.8 2.0 %collective-permute-start.3 = (f32[8,1024]{1,0:T(8,128)S(1)}, f32[8,1024]{1,0:T(8,128)S(1)}, u32[]{:S(2)}, u32[]{:S(2)}) collective-permute-start(f32[8,1024]{1,0:T(8,128)S(1)} %get-tuple-element.16), channel_id=1, source_target_pairs={{8,0},{16,8},{24,16},{32,24},{40,32},{48,40},{56,48},{64,56},{72,6... | collective-permute-start | bytes 98312 | tf_op jit(solution)/shard_map/ppermute | solution.py:624
  61.9 0.0 collective-permute-done.2.above
  61.9 6.2 %collective-permute-done.3.below = f32[8,1024]{1,0:T(8,128)S(1)} collective-permute-done((f32[8,1024]{1,0:T(8,128)S(1)}, f32[8,1024]{1,0:T(8,128)S(1)}, u32[]{:S(2)}, u32[]{:S(2)}) %collective-permute-start.3) | collective-permute-done | bytes 32800 | tf_op jit(solution)/shard_map/ppermute | solution.py:624
  68.1 3.0 %pack.1 = (f32[40,128]{1,0:T(8,128)S(1)}, f32[40,128]{1,0:T(8,128)S(1)}) custom-call(s32[16,3,32]{2,1,0:T(4,128)S(1)} %all_to_all.10.table, f32[512,1024]{1,0:T(8,128)} %a_in.3, f32[512,1024]{1,0:T(8,128)} %b_in.3, f32[512,1024]{1,0:T(8,128)} %l_in.3, f32[8,1024]{1,0:T(8,128)S(1)} %collective-permute-done.2.above, f32[8,1024]{1,0:T(8,128)S(1)} %collective-permute-done.3.below), custom_call_target="tpu_custom_call" | custom-call | tf_op jit(solution)/shard_map/pack/pallas_call | solution.py:641
  71.0 1.9 %collective-permute-start.4 = (f32[40,128]{1,0:T(8,128)S(1)}, f32[40,128]{1,0:T(8,128)S(1)}, u32[]{:S(2)}, u32[]{:S(2)}) collective-permute-start(f32[40,128]{1,0:T(8,128)S(1)} %get-tuple-element.17), channel_id=1, source_target_pairs={{1,0},{2,1},{3,2},{4,3},{5,4},{6,5},{7,6},{9,8},{10,9},{11,10},{12... | collective-permute-start | bytes 61448 | tf_op jit(solution)/shard_map/ppermute | solution.py:650
  73.0 0.0 copy-start
  73.0 0.0 copy-start.1
  73.0 2.5 %collective-permute-start.5 = (f32[40,128]{1,0:T(8,128)S(1)}, f32[40,128]{1,0:T(8,128)S(1)}, u32[]{:S(2)}, u32[]{:S(2)}) collective-permute-start(f32[40,128]{1,0:T(8,128)S(1)} %get-tuple-element.18), channel_id=1, source_target_pairs={{0,1},{1,2},{2,3},{3,4},{4,5},{5,6},{6,7},{8,9},{9,10},{10,11},{11... | collective-permute-start | bytes 61448 | tf_op jit(solution)/shard_map/ppermute | solution.py:651
  75.5 0.0 collective-permute-done.4.from_right
  75.5 2.7 %collective-permute-done.5.from_left = f32[40,128]{1,0:T(8,128)S(1)} collective-permute-done((f32[40,128]{1,0:T(8,128)S(1)}, f32[40,128]{1,0:T(8,128)S(1)}, u32[]{:S(2)}, u32[]{:S(2)}) %collective-permute-start.5) | collective-permute-done | bytes 20512 | tf_op jit(solution)/shard_map/ppermute | solution.py:651
  78.2 14.1 %prep_kernel.1.k_in = f32[5,9,552,128]{3,2,1,0:T(8,128)} custom-call(s32[16,3,32]{2,1,0:T(4,128)S(1)} %all_to_all.10.table, f32[512,1024]{1,0:T(8,128)} %a_in.3, f32[512,1024]{1,0:T(8,128)} %b_in.3, f32[512,1024]{1,0:T(8,128)} %l_in.3, f32[8,1024]{1,0:T(8,128)S(1)} %collective-permute-done.2.above, f32[8,1024]{1,0:T(8,128)S(1)} %collective-permute-done.3.below, ...), custom_call_target="tpu_custom_call" | custom-call | tf_op jit(solution)/shard_map/prep_kernel/pallas_call | solution.py:652
  92.3 0.0 collective-permute-done.from_right
  92.3 0.0 collective-permute-done.1.from_left
  92.3 0.0 copy-done
  92.4 0.0 copy-done.1
  92.4 12.8 %finish.1 = f32[512,1024]{1,0:T(8,128)} custom-call(bf16[384,256]{1,0:T(8,128)(2,1)S(1)} %copy-done, bf16[384,128]{1,0:T(8,128)(2,1)S(1)} %copy-done.1, f32[272,128]{1,0:T(8,128)S(1)} %get-tuple-element.12.left, f32[2,272,128]{2,1,0:T(8,128)S(1)} %get-tuple-element.13.middle, f32[272,128]{1,0:T(8,128)S(1)} %get-tuple-element.14.right, ...), custom_call_target="tpu_custom_call" | custom-call | tf_op jit(solution)/shard_map/finish/pallas_call | solution.py:684
  (1 shorter events, 0.0 us)
Async XLA Ops:
  50.8 41.6 %collective-permute-start = (f32[272,128]{1,0:T(8,128)S(1)}, f32[272,128]{1,0:T(8,128)S(1)}, u32[]{:S(2)}, u32[]{:S(2)}) collective-permute-start(f32[272,128]{1,0:T(8,128)S(1)} %get-tuple-element.12.left), channel_id=1, source_target_pairs={{1,0},{2,1},{3,2},{4,3},{5,4},{6,5},{7,6},{9,8},{10,9},{11,10},{12... | collective-permute-start | bytes 417800 | tf_op jit(solution)/shard_map/ppermute | solution.py:681
  52.7 39.6 %collective-permute-start.1 = (f32[272,128]{1,0:T(8,128)S(1)}, f32[272,128]{1,0:T(8,128)S(1)}, u32[]{:S(2)}, u32[]{:S(2)}) collective-permute-start(f32[272,128]{1,0:T(8,128)S(1)} %get-tuple-element.14.right), channel_id=1, source_target_pairs={{0,1},{1,2},{2,3},{3,4},{4,5},{5,6},{6,7},{8,9},{9,10},{10,11},{11... | collective-permute-start | bytes 417800 | tf_op jit(solution)/shard_map/ppermute | solution.py:682
  56.0 5.9 %collective-permute-start.2 = (f32[8,1024]{1,0:T(8,128)S(1)}, f32[8,1024]{1,0:T(8,128)S(1)}, u32[]{:S(2)}, u32[]{:S(2)}) collective-permute-start(f32[8,1024]{1,0:T(8,128)S(1)} %get-tuple-element.15), channel_id=1, source_target_pairs={{0,8},{8,16},{16,24},{24,32},{32,40},{40,48},{48,56},{56,64},{64,7... | collective-permute-start | bytes 98312 | tf_op jit(solution)/shard_map/ppermute | solution.py:623
  59.8 8.2 %collective-permute-start.3 = (f32[8,1024]{1,0:T(8,128)S(1)}, f32[8,1024]{1,0:T(8,128)S(1)}, u32[]{:S(2)}, u32[]{:S(2)}) collective-permute-start(f32[8,1024]{1,0:T(8,128)S(1)} %get-tuple-element.16), channel_id=1, source_target_pairs={{8,0},{16,8},{24,16},{32,24},{40,32},{48,40},{56,48},{64,56},{72,6... | collective-permute-start | bytes 98312 | tf_op jit(solution)/shard_map/ppermute | solution.py:624
  71.0 4.5 %collective-permute-start.4 = (f32[40,128]{1,0:T(8,128)S(1)}, f32[40,128]{1,0:T(8,128)S(1)}, u32[]{:S(2)}, u32[]{:S(2)}) collective-permute-start(f32[40,128]{1,0:T(8,128)S(1)} %get-tuple-element.17), channel_id=1, source_target_pairs={{1,0},{2,1},{3,2},{4,3},{5,4},{6,5},{7,6},{9,8},{10,9},{11,10},{12... | collective-permute-start | bytes 61448 | tf_op jit(solution)/shard_map/ppermute | solution.py:650
  73.0 19.4 %copy-start = (bf16[384,256]{1,0:T(8,128)(2,1)S(1)}, bf16[384,256]{1,0:T(8,128)(2,1)}, u32[]{:S(2)}) copy-start(bf16[384,256]{1,0:T(8,128)(2,1)} %constant.6.clone.group_weights) | copy-start | bytes 589828
  73.0 19.4 %copy-start.1 = (bf16[384,128]{1,0:T(8,128)(2,1)S(1)}, bf16[384,128]{1,0:T(8,128)(2,1)}, u32[]{:S(2)}) copy-start(bf16[384,128]{1,0:T(8,128)(2,1)} %constant.7.clone.side_weights) | copy-start | bytes 294916
  73.0 5.2 %collective-permute-start.5 = (f32[40,128]{1,0:T(8,128)S(1)}, f32[40,128]{1,0:T(8,128)S(1)}, u32[]{:S(2)}, u32[]{:S(2)}) collective-permute-start(f32[40,128]{1,0:T(8,128)S(1)} %get-tuple-element.18), channel_id=1, source_target_pairs={{0,1},{1,2},{2,3},{3,4},{4,5},{5,6},{6,7},{8,9},{9,10},{10,11},{11... | collective-permute-start | bytes 61448 | tf_op jit(solution)/shard_map/ppermute | solution.py:651
